TPU v7x, 256 devices: a whole 4x4x8 slice. The times are simulated.
256 devices in a mesh: req: 4 (over x), exp: 64 (over z, y, core).
Axes of the slice: x: 4, y: 4, z: 8, core: 2. Of those that a mesh axis runs over, the one named last changes fastest.
Arguments:
- hidden: bfloat16 [256, 32, 2048], P(('req', 'exp')), may hold values from -6 to 6
- queries: bfloat16 [256, 32, 3072], P(('req', 'exp'))
- new_latent: bfloat16 [256, 32, 576], P(('req', 'exp')), may hold values from -6 to 6
- pages: bfloat16 [2048, 128, 576], P(('req', 'exp'))
- page_table: int32 [256, 8], P(('req', 'exp')), may hold values from 0 to 7, each once within a row
- cache_len: int32 [256], P(('req', 'exp')), may hold values from 1 to 992, as said below
- parents: int32 [256, 32], P(('req', 'exp')), may hold values from 0 to 30, as said below
- accept_path: int32 [256, 32], P(('req', 'exp')), may hold values from 0 to 31, as said below
- accept_count: int32 [256], P(('req', 'exp')), may hold values from 1 to 32, as said below
- key_up: bfloat16 [16, 128, 512], replicated, may hold values from -0.5 to 0.5
- value_up: bfloat16 [16, 512, 128], replicated, may hold values from -0.25 to 0.25
- out_proj: bfloat16 [2048, 2048], P(None, 'req'), may hold values from -0.125 to 0.125
- norm_gain: bfloat16 [2048], replicated, may hold values from 0.5 to 1.5
- route_ids: int32 [4, 64, 32, 6], P(None, 'exp'), may hold values from 0 to 63, all different within a row; in each aligned block of 32 rows (0 to 31, 32 to 63, ..., all dimensions but the last counted through in order) at most 6 rows name the same one
- route_weights: float32 [4, 64, 32, 6], P(None, 'exp'), may hold values from 0.2 to 1.2
- w_gate: bfloat16 [64, 2048, 1408], P('exp', None, 'req'), may hold values from -0.125 to 0.125
- w_up: bfloat16 [64, 2048, 1408], P('exp', None, 'req'), may hold values from -0.125 to 0.125
- w_down: bfloat16 [64, 1408, 2048], P('exp', 'req'), may hold values from -0.15625 to 0.15625
Outputs:
- layer_out: bfloat16 [256, 32, 2048], P(('req', 'exp'))
- new_pages: bfloat16 [2048, 128, 576], P(('req', 'exp'))
Inputs may be any that keep to these rules, and one draw needn't show every extreme that they name: `route_ids`: in each request no expert is named by more than 6 tokens, a bound that some block reaches. `page_table`: each row is an order of the 8 pages of the request's pool. `cache_len`: some request holds the largest length. parents[q, 0] = 0; for t >= 1 the parent of t is below t; one request's tree is a single chain. `accept_path`: entry k for k < accept_count is the ancestor at depth k of the last accepted token, entry 0 the root; later entries are 0. `accept_count`: one more than the depth of the last accepted token.
All inputs are finite; a program needn't handle non-finite values.
Results may differ from a plain program's by a relative error of at most 0.023.
Values may be sent and summed in bfloat16 or wider, within the bound.
A program may use at most 128 MiB of HBM per device.

v0:
```python
import math

import jax
import jax.numpy as jnp
from jax import lax
from jax.sharding import PartitionSpec as P

TOP = 6
TREE = 32


def ancestry(parent_row):
    count = parent_row.shape[0]
    ident = jnp.eye(count, dtype=jnp.int32)
    linked = (parent_row[:, None] == jnp.arange(count, dtype=jnp.int32)[None, :]).astype(jnp.int32)
    reach = jnp.minimum(ident + linked, 1)
    for sweep in range(count.bit_length()):
        reach = jnp.minimum(jnp.dot(reach, reach), 1)
    return reach


def attend(query_row, page_pool, table_row, length, parent_row, fresh, key_up, value_up):
    count = query_row.shape[0]
    heads = key_up.shape[0]
    nope = key_up.shape[1]
    latent = key_up.shape[2]
    shaped = query_row.reshape(count, heads, -1)
    scale = 1.0 / math.sqrt(shaped.shape[2])
    q_nope = shaped[:, :, :nope]
    q_rope = shaped[:, :, nope:]
    q_latent = jnp.einsum(
        "thn,hnc->thc", q_nope, key_up, preferred_element_type=jnp.float32
    ).astype(jnp.bfloat16)
    q_full = jnp.concatenate([q_latent, q_rope], axis=2)
    cache_rows = jnp.take(page_pool, table_row, axis=0).reshape(-1, page_pool.shape[2])
    score_cache = (
        jnp.einsum("thc,kc->thk", q_full, cache_rows, preferred_element_type=jnp.float32) * scale
    )
    score_tree = (
        jnp.einsum("thc,jc->thj", q_full, fresh, preferred_element_type=jnp.float32) * scale
    )
    live = jnp.arange(cache_rows.shape[0], dtype=jnp.int32) < length
    score_cache = jnp.where(live[None, None, :], score_cache, -1e30)
    score_tree = jnp.where(ancestry(parent_row)[:, None, :] > 0, score_tree, -1e30)
    peak = jnp.maximum(jnp.max(score_cache, axis=2), jnp.max(score_tree, axis=2))[:, :, None]
    exp_cache = jnp.exp(score_cache - peak)
    exp_tree = jnp.exp(score_tree - peak)
    total = jnp.sum(exp_cache, axis=2, keepdims=True) + jnp.sum(exp_tree, axis=2, keepdims=True)
    prob_cache = (exp_cache / total).astype(jnp.bfloat16)
    prob_tree = (exp_tree / total).astype(jnp.bfloat16)
    context = jnp.einsum(
        "thk,kc->thc", prob_cache, cache_rows[:, :latent], preferred_element_type=jnp.float32
    )
    context = context + jnp.einsum(
        "thj,jc->thc", prob_tree, fresh[:, :latent], preferred_element_type=jnp.float32
    )
    context = context.astype(jnp.bfloat16)
    head_out = jnp.einsum(
        "thc,hcv->thv", context, value_up, preferred_element_type=jnp.float32
    ).astype(jnp.bfloat16)
    return head_out.reshape(count, -1)


def write_rows(page_pool, table_row, length, path_row, count, fresh):
    pool_len = page_pool.shape[0]
    page_size = page_pool.shape[1]
    pool_ids = jnp.arange(pool_len, dtype=jnp.int32)
    match = table_row[None, :] == pool_ids[:, None]
    logical = jnp.sum(jnp.where(match, pool_ids[None, :], 0), axis=1)
    position = logical[:, None] * page_size + jnp.arange(page_size, dtype=jnp.int32)[None, :]
    offset = position - length
    valid = (offset >= 0) & (offset < count)
    source = jnp.take(path_row, jnp.clip(offset, 0, path_row.shape[0] - 1))
    written = jnp.take(fresh, source, axis=0)
    return jnp.where(valid[:, :, None], written, page_pool)


def slot_tables(route_rows, weight_rows, experts, capacity):
    expert_ids = jnp.arange(experts, dtype=jnp.int32)
    hits = route_rows[:, :, :, None] == expert_ids
    chosen = jnp.sum(hits.astype(jnp.int32), axis=2)
    weight_by = jnp.sum(jnp.where(hits, weight_rows[:, :, :, None], 0.0), axis=2)
    before = jnp.cumsum(chosen, axis=1) - chosen
    chosen_t = jnp.transpose(chosen, (0, 2, 1))
    before_t = jnp.transpose(before, (0, 2, 1))
    weight_t = jnp.transpose(weight_by, (0, 2, 1))
    slot_ids = jnp.arange(capacity, dtype=jnp.int32)
    placed = (chosen_t[:, :, None, :] > 0) & (
        before_t[:, :, None, :] == slot_ids[None, None, :, None]
    )
    weighted = jnp.where(placed, weight_t[:, :, None, :], 0.0)
    return (placed.astype(jnp.bfloat16), weighted)


def local(
    hidden,
    queries,
    new_latent,
    pages,
    page_table,
    cache_len,
    parents,
    accept_path,
    accept_count,
    key_up,
    value_up,
    out_proj,
    norm_gain,
    route_ids,
    route_weights,
    w_gate,
    w_up,
    w_down,
):
    width = hidden.shape[2]
    head_out = attend(
        queries[0], pages, page_table[0], cache_len[0], parents[0], new_latent[0], key_up, value_up
    )
    column_block = jnp.dot(
        lax.all_gather(head_out, "req", axis=0, tiled=True),
        out_proj,
        preferred_element_type=jnp.float32,
    ).astype(jnp.bfloat16)
    projected = lax.all_to_all(column_block, "req", split_axis=0, concat_axis=1, tiled=True)
    mixed = (hidden[0].astype(jnp.float32) + projected.astype(jnp.float32)).astype(jnp.bfloat16)
    mixed_f = mixed.astype(jnp.float32)
    normed = (
        mixed_f
        * lax.rsqrt(jnp.mean(mixed_f * mixed_f, axis=1, keepdims=True) + 1e-06)
        * norm_gain.astype(jnp.float32)
    ).astype(jnp.bfloat16)
    experts = lax.axis_size("exp") * w_gate.shape[0]
    capacity = max(2, min(TREE, 2 * TREE * TOP // experts))
    gate_local = w_gate[0]
    up_local = w_up[0]
    down_local = w_down[0]
    copies = lax.all_gather(normed[None], "req", axis=0, tiled=True)
    placed, weighted = slot_tables(route_ids[:, 0], route_weights[:, 0], experts, capacity)
    outbound = jnp.einsum(
        "gxct,gtd->xgcd", placed, copies, preferred_element_type=jnp.float32
    ).astype(jnp.bfloat16)
    slot_block = lax.all_to_all(outbound, "exp", split_axis=0, concat_axis=0, tiled=True)
    flat = slot_block.reshape(-1, width)
    gate_val = jnp.dot(flat, gate_local, preferred_element_type=jnp.float32)
    up_val = jnp.dot(flat, up_local, preferred_element_type=jnp.float32)
    active = (jax.nn.silu(gate_val) * up_val).astype(jnp.bfloat16)
    returned = lax.all_to_all(
        jnp.dot(active, down_local, preferred_element_type=jnp.float32)
        .astype(jnp.bfloat16)
        .reshape(slot_block.shape),
        "exp",
        split_axis=0,
        concat_axis=0,
        tiled=True,
    )
    partial_value = jnp.einsum("gxct,xgcd->gtd", weighted, returned.astype(jnp.float32))
    moe = lax.psum_scatter(
        partial_value.astype(jnp.bfloat16), "req", scatter_dimension=0, tiled=True
    ).astype(jnp.float32)[0]
    layer_out = (mixed_f + moe).astype(jnp.bfloat16)[None]
    new_pool = write_rows(
        pages, page_table[0], cache_len[0], accept_path[0], accept_count[0], new_latent[0]
    )
    return (layer_out, new_pool)


def solution(mesh):
    in_specs = (
        P(("req", "exp"), None, None),
        P(("req", "exp"), None, None),
        P(("req", "exp"), None, None),
        P(("req", "exp"), None, None),
        P(("req", "exp"), None),
        P(("req", "exp")),
        P(("req", "exp"), None),
        P(("req", "exp"), None),
        P(("req", "exp")),
        P(),
        P(),
        P(None, "req"),
        P(),
        P(None, "exp", None, None),
        P(None, "exp", None, None),
        P("exp", None, "req"),
        P("exp", None, "req"),
        P("exp", "req", None),
    )
    out_specs = (P(("req", "exp"), None, None), P(("req", "exp"), None, None))
    return jax.shard_map(local, mesh=mesh, in_specs=in_specs, out_specs=out_specs, check_vma=False)
```

profile of v0, /device:TPU:1, one launch (start us, length us, event | category | flops | bytes accessed | tf_op | source)
XLA Modules:
  0.0 495.2 jit_solution(1943214140383278034)
XLA Ops:
  13.1 2.4 copy.166
  17.3 2.4 fusion.9
  28.1 2.5 fusion.22
  30.7 12.3 %all_gather.6 = bf16[128,2048]{1,0:T(8,128)(2,1)S(1)} all-gather(bf16[32,2048]{1,0:T(8,128)(2,1)S(1)} %bitcast.125), channel_id=1, replica_groups=mesh['req'=4,'exp'=64] {'req'}, dimensions={0}, use_global_device_ids=true | all-gather | bytes 655360 | tf_op jit(solution)/shard_map/all_gather | solution.py:120
  43.0 2.7 convolution_convert_fusion.2
  45.7 3.5 all-to-all-start
  49.5 4.4 all-to-all-done
  54.7 10.2 %all_gather.7 = bf16[4,32,2048]{2,1,0:T(8,128)(2,1)S(1)} all-gather(bf16[1,32,2048]{2,1,0:T(8,128)(2,1)S(1)} %fusion.38), channel_id=1, replica_groups=mesh['req'=4,'exp'=64] {'req'}, dimensions={0}, use_global_device_ids=true | all-gather | bytes 655360 | tf_op jit(solution)/shard_map/all_gather | solution.py:137
  64.8 4.5 convert_bitcast_fusion
  69.3 10.3 %copy.157 = bf16[64,4,6,2048]{3,1,2,0:T(4,128)(2,1)} copy(bf16[64,4,6,2048]{3,0,2,1:T(8,128)(2,1)} %convert_bitcast_fusion) | data formatting | bytes 12582912 | tf_op jit(solution)/shard_map/convert_element_type | solution.py:141
  79.6 159.3 %all_to_all.23 = bf16[64,4,6,2048]{3,1,2,0:T(4,128)(2,1)S(1)} all-to-all(bf16[64,4,6,2048]{3,1,2,0:T(4,128)(2,1)} %copy.157), channel_id=1, replica_groups=mesh['req'=4,'exp'=64] {'exp'}, dimensions={0} | all-to-all | bytes 12582912 | tf_op jit(solution)/shard_map/all_to_all | solution.py:142
  239.0 10.7 %copy.158 = bf16[64,4,6,2048]{3,2,1,0:T(8,128)(2,1)} copy(bf16[64,4,6,2048]{3,1,2,0:T(4,128)(2,1)S(1)} %all_to_all.23) | data formatting | bytes 12582912 | tf_op jit(solution)/shard_map/all_to_all | solution.py:142
  249.7 11.1 %reshape.257 = bf16[1536,2048]{1,0:T(8,128)(2,1)} reshape(bf16[64,4,6,2048]{3,2,1,0:T(8,128)(2,1)} %copy.158) | data formatting | bytes 12582912 | tf_op jit(solution)/shard_map/reshape | solution.py:143
  260.7 7.0 %fusion.13 = f32[1536,352]{0,1:T(8,128)} fusion(bf16[1536,2048]{1,0:T(8,128)(2,1)} %reshape.257, bf16[1,2048,352]{1,2,0:T(8,128)(2,1)} %param.33), kind=kOutput, calls=%fused_computation.18 | convolution fusion | flops 2214592512 | bytes 9895936 | tf_op jit(solution)/shard_map/dot_general | solution.py:144
  267.7 12.2 %convolution_convert_fusion = bf16[1536,2048]{1,0:T(8,128)(2,1)} fusion(bf16[1,352,2048]{2,1,0:T(8,128)(2,1)} %param.35, bf16[1536,2048]{1,0:T(8,128)(2,1)} %reshape.257, f32[1536,352]{0,1:T(8,128)} %fusion.13, bf16[1,2048,352]{1,2,0:T(8,128)(2,1)} %param.34), kind=kOutput, calls=%fused_computation.3 | convolution fusion | flops 4435574784 | bytes 17629184 | tf_op jit(solution)/shard_map/dot_general | solution.py:148
  279.9 11.4 %reshape.258 = bf16[64,4,6,2048]{3,2,1,0:T(8,128)(2,1)} reshape(bf16[1536,2048]{1,0:T(8,128)(2,1)} %convolution_convert_fusion) | data formatting | bytes 12582912 | tf_op jit(solution)/shard_map/reshape | solution.py:150
  291.3 18.8 %copy.159 = bf16[64,4,6,2048]{3,1,2,0:T(4,128)(2,1)} copy(bf16[64,4,6,2048]{3,2,1,0:T(8,128)(2,1)} %reshape.258) | data formatting | bytes 12582912 | tf_op jit(solution)/shard_map/reshape | solution.py:150
  310.1 7.3 %all-to-all-start.2 = ((bf16[64,4,6,2048]{3,1,2,0:T(4,128)(2,1)}), bf16[64,4,6,2048]{3,1,2,0:T(4,128)(2,1)}, u32[]{:S(2)}, u32[]{:S(2)}) async-start(bf16[64,4,6,2048]{3,1,2,0:T(4,128)(2,1)} %copy.159), calls=%async_computation.2 | async-start | bytes 12582912 | tf_op jit(solution)/shard_map/all_to_all | solution.py:147
  317.9 138.3 %all-to-all-done.2 = bf16[64,4,6,2048]{3,1,2,0:T(4,128)(2,1)} async-done(((bf16[64,4,6,2048]{3,1,2,0:T(4,128)(2,1)}), bf16[64,4,6,2048]{3,1,2,0:T(4,128)(2,1)}, u32[]{:S(2)}, u32[]{:S(2)}) %all-to-all-start.2) | async-done | bytes 6291488 | tf_op jit(solution)/shard_map/all_to_all | solution.py:147
  456.2 10.5 %fusion.6 = bf16[4,32,2048]{2,1,0:T(8,128)(2,1)} fusion(bf16[64,4,6,2048]{3,1,2,0:T(4,128)(2,1)} %all-to-all-done.2, bf16[4,64,32]{1,2,0:T(8,128)(2,1)S(1)} %bitcast.128, s32[4,64,32]{1,2,0:T(8,128)S(1)} %subtract_bitcast_fusion, pred[4,64,32]{1,2,0:T(8,128)(4,1)S(1)} %compare_bitcast_fusion), kind=kOutput, calls=%fused_computation.10 | convolution fusion | flops 201474048 | bytes 6873088 | tf_op jit(solution)/shard_map/gxct,xgcd->gtd/dot_general | solution.py:156
  467.4 6.6 %gather_fusion.1 = s32[1024]{0:T(1024)S(1)} fusion(s32[32]{0:T(128)S(1)} %bitcast.120, s32[1024]{0:T(1024)S(1)} %bitcast_clamp_fusion), kind=kCustom, calls=%fused_computation.1 | custom fusion | bytes 12288 | tf_op jit(solution)/shard_map/jit(_take)/gather | solution.py:73
  474.0 4.0 gather_fusion.2
  480.2 2.6 select_select_fusion
  482.8 3.6 reduce-scatter.2.cloned.1.call-done
  (89 shorter events, 20.6 us)
Async XLA Ops:
  7.2 8.4 %copy-start = (bf16[16,128,512]{2,1,0:T(8,128)(2,1)S(1)}, bf16[16,128,512]{2,1,0:T(8,128)(2,1)}, u32[]{:S(2)}) copy-start(bf16[16,128,512]{2,1,0:T(8,128)(2,1)} %param.27) | copy-start | bytes 6291460
  7.2 4.2 copy-start.4
  11.3 4.7 copy-start.9
  11.4 4.2 copy-start.11
  15.5 1.4 copy-start.5
  16.0 0.8 copy-start.6
  17.2 2.5 copy-start.15
  17.2 3.7 copy-start.3
  17.2 3.7 copy-start.7
  17.3 3.7 copy-start.10
  30.6 18.5 %copy-start.12 = (s32[4,1,32,6]{2,1,3,0:T(1,128)S(1)}, s32[4,1,32,6]{2,1,3,0:T(1,128)}, u32[]{:S(2)}) copy-start(s32[4,1,32,6]{2,1,3,0:T(1,128)} %param.31) | copy-start | bytes 9220
  30.6 18.8 %copy-start.14 = (bf16[2048]{0:T(1024)(128)(2,1)S(1)}, bf16[2048]{0:T(1024)(128)(2,1)}, u32[]{:S(2)}) copy-start(bf16[2048]{0:T(1024)(128)(2,1)} %param.30) | copy-start | bytes 12292
  45.7 8.7 %copy-start.8 = (bf16[1,32,2048]{2,1,0:T(8,128)(2,1)S(1)}, bf16[1,32,2048]{2,1,0:T(8,128)(2,1)}, u32[]{:S(2)}) copy-start(bf16[1,32,2048]{2,1,0:T(8,128)(2,1)} %param.18) | copy-start | bytes 393220
  45.7 8.3 %all-to-all-start = ((bf16[4,32,512]{2,1,0:T(8,128)(2,1)}), bf16[4,32,512]{2,1,0:T(8,128)(2,1)S(1)}, u32[]{:S(2)}, u32[]{:S(2)}) async-start(bf16[4,32,512]{2,1,0:T(8,128)(2,1)} %bitcast.14), calls=%async_computation | async-start | bytes 262144 | tf_op jit(solution)/shard_map/all_to_all | solution.py:124
  310.1 7.4 %copy-start.13 = (f32[4,1,32,6]{2,1,3,0:T(1,128)S(1)}, f32[4,1,32,6]{2,1,3,0:T(1,128)}, u32[]{:S(2)}) copy-start(f32[4,1,32,6]{2,1,3,0:T(1,128)} %param.32) | copy-start | bytes 9220
  310.1 7.4 %copy-start.16 = (s32[1,8]{1,0:T(1,128)S(1)}, s32[1,8]{1,0:T(1,128)}, u32[]{:S(2)}) copy-start(s32[1,8]{1,0:T(1,128)} %param.22) | copy-start | bytes 100
  310.1 146.1 %all-to-all-start.2 = ((bf16[64,4,6,2048]{3,1,2,0:T(4,128)(2,1)}), bf16[64,4,6,2048]{3,1,2,0:T(4,128)(2,1)}, u32[]{:S(2)}, u32[]{:S(2)}) async-start(bf16[64,4,6,2048]{3,1,2,0:T(4,128)(2,1)} %copy.159), calls=%async_computation.2 | async-start | bytes 12582912 | tf_op jit(solution)/shard_map/all_to_all | solution.py:147
  317.5 169.0 %reduce-scatter.2.cloned.1.call-start = ((), (), s32[]{:S(2)}) async-start(), calls=%async_computation.4 | async-start | bytes 655360 | tf_op jit(solution)/shard_map/reduce_scatter | solution.py:157
  466.7 0.7 copy-start.2
  480.2 7.9 %copy-start.1 = (bf16[16,128,512]{2,1,0:T(8,128)(2,1)S(1)}, bf16[16,128,512]{2,1,0:T(8,128)(2,1)}, u32[]{:S(2)}) copy-start(bf16[16,128,512]{2,1,0:T(8,128)(2,1)} %param.27) | copy-start | bytes 6291460
Sparse Core Ops, SparseCore 0:
  466.9 19.5 reduce-scatter.1
where the time goes:
time: 503 us; the launch traced here: 495 us
  blocking collectives  182 us (36%)
  waiting for transfers between devices  146 us (29%)
  local copies, waits for them, and re-layouts  82.9 us (16%)
  matrix products  45.8 us (9%)
  between operations  16 us (3%)
  other arithmetic  11.5 us (2%)
  starting transfers between devices  10.8 us (2%)
    all_to_all x1, blocking collectives, local(): lax.all_to_all(outbound, 'exp', split_axis=0, concat_axis=0, tiled=True)  159 us
    all_to_all x1, waiting for transfers between devices, local(): lax.all_to_all(jnp.dot(active, down_local, preferred_element_type=jnp.flo...  138 us
    reshape x2, local copies, waits for them, and re-layouts, local(): returned = lax.all_to_all(jnp.dot(active, down_local, preferred_element_t...  30.2 us
    all_gather x1, blocking collectives, local(): lax.all_gather(head_out, 'req', axis=0, tiled=True)  12.3 us
    dot_general x1, matrix products, local(): jnp.dot(active, down_local, preferred_element_type=jnp.float32)  12.2 us
    reshape x1, local copies, waits for them, and re-layouts, local(): flat = slot_block.reshape(-1, width)  11.1 us
    all_to_all x1, local copies, waits for them, and re-layouts, local(): lax.all_to_all(outbound, 'exp', split_axis=0, concat_axis=0, tiled=True)  10.7 us
    dot_general x1, matrix products, local(): jnp.einsum('gxct,xgcd->gtd', weighted, returned.astype(jnp.float32))  10.5 us
  transfers between devices with their start and end apart: 3, of which 3 were waited for; matrix products, arithmetic and copies ran while one was open for 3% of the time, Pallas kernels for 0%

commit v1 on v0

v1 whole, which is shorter than its diff:
```python
import functools
import math

import jax
import jax.numpy as jnp
from jax import lax
from jax.experimental import pallas as pl
from jax.experimental.pallas import tpu as pltpu
from jax.sharding import PartitionSpec as P

MESH = pl.DeviceIdType.MESH
TOP = 6
TREE = 32
NX = 4
NY = 4
NZ = 8
CHUNKS = 4
F32 = jnp.float32
BF16 = jnp.bfloat16


def ancestry(parent_row):
    count = parent_row.shape[0]
    ident = jnp.eye(count, dtype=jnp.int32)
    linked = (parent_row[:, None] == jnp.arange(count, dtype=jnp.int32)[None, :]).astype(jnp.int32)
    reach = jnp.minimum(ident + linked, 1)
    for sweep in range(count.bit_length()):
        reach = jnp.minimum(jnp.dot(reach, reach), 1)
    return reach


def attend(query_row, page_pool, table_row, length, parent_row, fresh, key_up, value_up):
    count = query_row.shape[0]
    heads = key_up.shape[0]
    nope = key_up.shape[1]
    latent = key_up.shape[2]
    shaped = query_row.reshape(count, heads, -1)
    scale = 1.0 / math.sqrt(shaped.shape[2])
    q_nope = shaped[:, :, :nope]
    q_rope = shaped[:, :, nope:]
    q_latent = jnp.einsum("thn,hnc->thc", q_nope, key_up, preferred_element_type=F32).astype(BF16)
    q_full = jnp.concatenate([q_latent, q_rope], axis=2)
    cache_rows = jnp.take(page_pool, table_row, axis=0).reshape(-1, page_pool.shape[2])
    score_cache = jnp.einsum("thc,kc->thk", q_full, cache_rows, preferred_element_type=F32) * scale
    score_tree = jnp.einsum("thc,jc->thj", q_full, fresh, preferred_element_type=F32) * scale
    live = jnp.arange(cache_rows.shape[0], dtype=jnp.int32) < length
    score_cache = jnp.where(live[None, None, :], score_cache, -1e30)
    score_tree = jnp.where(ancestry(parent_row)[:, None, :] > 0, score_tree, -1e30)
    peak = jnp.maximum(jnp.max(score_cache, axis=2), jnp.max(score_tree, axis=2))[:, :, None]
    exp_cache = jnp.exp(score_cache - peak)
    exp_tree = jnp.exp(score_tree - peak)
    total = jnp.sum(exp_cache, axis=2, keepdims=True) + jnp.sum(exp_tree, axis=2, keepdims=True)
    prob_cache = (exp_cache / total).astype(BF16)
    prob_tree = (exp_tree / total).astype(BF16)
    context = jnp.einsum("thk,kc->thc", prob_cache, cache_rows[:, :latent], preferred_element_type=F32)
    context = context + jnp.einsum("thj,jc->thc", prob_tree, fresh[:, :latent], preferred_element_type=F32)
    context = context.astype(BF16)
    head_out = jnp.einsum("thc,hcv->thv", context, value_up, preferred_element_type=F32).astype(BF16)
    return head_out.reshape(count, -1)


def write_rows(page_pool, table_row, length, path_row, count, fresh):
    pool_len = page_pool.shape[0]
    page_size = page_pool.shape[1]
    pool_ids = jnp.arange(pool_len, dtype=jnp.int32)
    match = table_row[None, :] == pool_ids[:, None]
    logical = jnp.sum(jnp.where(match, pool_ids[None, :], 0), axis=1)
    position = logical[:, None] * page_size + jnp.arange(page_size, dtype=jnp.int32)[None, :]
    offset = position - length
    valid = (offset >= 0) & (offset < count)
    steps = jnp.arange(path_row.shape[0], dtype=jnp.int32)
    tokens = jnp.arange(fresh.shape[0], dtype=jnp.int32)
    by_step = jnp.dot(
        (path_row[:, None] == tokens[None, :]).astype(BF16), fresh, preferred_element_type=F32
    ).astype(BF16)
    pick = (offset.reshape(-1)[:, None] == steps[None, :]).astype(BF16)
    written = jnp.dot(pick, by_step, preferred_element_type=F32).astype(BF16)
    return jnp.where(valid[:, :, None], written.reshape(page_pool.shape), page_pool)


def slot_table(route_row, weight_row, expert_ids, capacity):
    hits = route_row[:, :, None] == expert_ids
    chosen = jnp.sum(hits.astype(jnp.int32), axis=1)
    weight_by = jnp.sum(jnp.where(hits, weight_row[:, :, None], 0.0), axis=1)
    tokens = route_row.shape[0]
    earlier = (jnp.arange(tokens)[:, None] > jnp.arange(tokens)[None, :]).astype(BF16)
    before = jnp.dot(earlier, chosen.astype(BF16), preferred_element_type=F32).astype(jnp.int32)
    chosen_t, before_t, weight_t = chosen.T, before.T, weight_by.T
    slot_ids = jnp.arange(capacity, dtype=jnp.int32)
    placed = (chosen_t[:, None, :] > 0) & (before_t[:, None, :] == slot_ids[None, :, None])
    weighted = jnp.where(placed, weight_t[:, None, :], 0.0)
    both = jnp.concatenate([placed.astype(BF16), weighted.astype(BF16)], axis=2)
    both = jnp.pad(both, ((0, 0), (0, 0), (0, 128 - 2 * tokens)))
    return both.reshape(NZ, -1, 128)


def layer_kernel(
    head_ref, hid_ref, gain_ref, tab_ref, perm_ref, spread_ref, mask_ref,
    oproj_hbm, wg_hbm, wu_hbm, wd_hbm,
    out_ref,
    oproj, wg, wu, wd, heads, po, co, mixed, tabs, sel, wt, tok, ysend, x, accg, accu, act,
    p, a1, a3, bl, br, zz, v, zsend, zrecv,
    w_sem, h_s, h_r, o_s, o_r, t_s, t_r, fz_s, fz_r, fy_s, fy_r, fx_s, fx_r,
    gx_s, gx_r, gy_s, gy_r, gz_s, gz_r,
):
    rx = lax.axis_index("req")
    e = lax.axis_index("exp")
    ez = e // (2 * NY)
    ey = (e // 2) % NY
    ec = e % 2
    width = hid_ref.shape[1]
    cc = width // CHUNKS
    slots = ysend.shape[2]
    rows = x.shape[2]
    half = rows // 2
    tree = hid_ref.shape[0]

    def at_x(k):
        return ((rx + k) % NX, e)

    def at_z(k):
        return (rx, (((ez + k) % NZ) * NY + ey) * 2 + ec)

    def at_y(d):
        return (rx, (ez * NY + (ey + d // 2) % NY) * 2 + (ec + d % 2) % 2)

    def flip_y(d):
        return ((NY - d // 2) % NY) * 2 + d % 2

    weights = [
        pltpu.make_async_copy(oproj_hbm, oproj, w_sem.at[0]),
        pltpu.make_async_copy(wg_hbm, wg, w_sem.at[1]),
        pltpu.make_async_copy(wu_hbm, wu, w_sem.at[2]),
        pltpu.make_async_copy(wd_hbm, wd, w_sem.at[3]),
    ]
    for copy in weights:
        copy.start()

    barrier = pltpu.get_barrier_semaphore()
    partners = (
        [at_x(k) for k in range(1, NX)]
        + [at_y(d) for d in range(1, 2 * NY)]
        + [at_z(k) for k in range(1, NZ)]
    )
    for partner in partners:
        pl.semaphore_signal(barrier, inc=1, device_id=partner, device_id_type=MESH)
    pl.semaphore_wait(barrier, len(partners))

    started = []

    def send(src, dst, ss, rs, device):
        copy = pltpu.make_async_remote_copy(
            src_ref=src, dst_ref=dst, send_sem=ss, recv_sem=rs, device_id=device, device_id_type=MESH
        )
        copy.start()
        started.append(copy)
        return copy

    head_copies = [
        send(head_ref, heads.at[NX - k], h_s.at[k], h_r.at[NX - k], at_x(k)) for k in (1, 3, 2)
    ]
    tab_copies = [
        send(tab_ref.at[k], tabs.at[NZ - k], t_s.at[k], t_r.at[NZ - k], at_z(k)) for k in range(1, NZ)
    ]
    heads[0] = head_ref[...]
    tabs[0] = tab_ref[0]
    weights[0].wait()
    for copy in head_copies:
        copy.wait_recv()
    proj = jnp.dot(heads[...].reshape(NX * tree, width), oproj[...], preferred_element_type=F32)
    po[...] = proj.astype(BF16).reshape(po.shape)
    back_copies = [send(po.at[k], co.at[rx], o_s.at[k], o_r.at[NX - k], at_x(k)) for k in (1, 3, 2)]
    co[rx] = po[0]
    for copy in tab_copies:
        copy.wait_recv()
    flat_tabs = tabs[...].reshape(NZ * slots, 128)
    wide = jnp.dot(flat_tabs, spread_ref[...], preferred_element_type=F32) * mask_ref[...].astype(F32)
    both = jnp.dot(perm_ref[...], wide.astype(BF16), preferred_element_type=F32)
    sel[...] = both[:, : NZ * tree].astype(BF16)
    wt[...] = both[:, NZ * tree :].T.astype(BF16)

    for copy in back_copies:
        copy.wait_recv()
    square = jnp.zeros((tree, 1), F32)
    for c in range(CHUNKS):
        m = (hid_ref[:, c * cc : (c + 1) * cc].astype(F32) + co[c].astype(F32)).astype(BF16)
        mixed[c] = m
        mf = m.astype(F32)
        square = square + jnp.sum(mf * mf, axis=1, keepdims=True)
    factor = lax.rsqrt(square * (1.0 / width) + 1e-06)

    fz, fy, fx, fw = {}, {}, {}, {}
    for c in range(CHUNKS):
        gain = gain_ref[:, c * cc : (c + 1) * cc].astype(F32)
        tok[c, 0] = (mixed[c].astype(F32) * factor * gain).astype(BF16)
        fz[c] = [
            send(tok.at[c, 0], tok.at[c, NZ - k], fz_s.at[c, k], fz_r.at[c, NZ - k], at_z(k))
            for k in (1, 7, 2, 6, 3, 5, 4)
        ]

    def select(c):
        for copy in fz[c]:
            copy.wait_recv()
        block = jnp.dot(sel[...], tok[c].reshape(NZ * tree, cc), preferred_element_type=F32)
        block = block.astype(BF16)
        x[c, 0, 0:slots] = block[0:slots]
        ysend[c] = block.reshape(2 * NY, slots, cc)
        fy[c] = [
            send(
                ysend.at[c, d],
                x.at[c, 0, pl.ds(flip_y(d) * slots, slots)],
                fy_s.at[c, d],
                fy_r.at[c, flip_y(d)],
                at_y(d),
            )
            for d in (1, 2, 6, 3, 7, 4, 5)
        ]

    def spread_x(c):
        for copy in fy[c]:
            copy.wait_recv()
        fx[c] = [
            send(x.at[c, 0], x.at[c, 3], fx_s.at[c, 0], fx_r.at[c, 0], at_x(1)),
            send(x.at[c, 0], x.at[c, 1], fx_s.at[c, 1], fx_r.at[c, 1], at_x(3)),
        ]

    def forward_x(c):
        top, bottom = pl.ds(0, half), pl.ds(half, half)
        fx[c][0].wait_recv()
        first = send(x.at[c, 3, top], x.at[c, 2, top], fx_s.at[c, 2], fx_r.at[c, 2], at_x(1))
        fx[c][1].wait_recv()
        second = send(x.at[c, 1, bottom], x.at[c, 2, bottom], fx_s.at[c, 3], fx_r.at[c, 3], at_x(3))
        fw[c] = [first, second]

    def expand(c):
        for copy in fw[c]:
            copy.wait_recv()
        if c == 0:
            weights[1].wait()
            weights[2].wait()

        def body(g, carry):
            block = x[c, g]
            gv = jnp.dot(block, wg[c * cc : (c + 1) * cc, :], preferred_element_type=F32)
            uv = jnp.dot(block, wu[c * cc : (c + 1) * cc, :], preferred_element_type=F32)
            if c > 0:
                gv = gv + accg[g]
                uv = uv + accu[g]
            if c == CHUNKS - 1:
                act[g] = (gv * jax.nn.sigmoid(gv) * uv).astype(BF16)
            else:
                accg[g] = gv
                accu[g] = uv
            return carry

        lax.fori_loop(0, NX, body, 0)

    for i in range(CHUNKS + 3):
        if i < CHUNKS:
            select(i)
        if 0 <= i - 1 < CHUNKS:
            spread_x(i - 1)
        if 0 <= i - 2 < CHUNKS:
            forward_x(i - 2)
        if 0 <= i - 3 < CHUNKS:
            expand(i - 3)

    weights[3].wait()
    gx, gw, gy, gz = {}, {}, {}, {}

    def contract(c):
        top, bottom = pl.ds(0, half), pl.ds(half, half)
        down = wd[:, c * cc : (c + 1) * cc]
        p[c, 2] = jnp.dot(act[2], down, preferred_element_type=F32).astype(BF16)
        gx[c] = [
            send(p.at[c, 2, top], a1.at[c], gx_s.at[c, 0], gx_r.at[c, 0], at_x(1)),
            send(p.at[c, 2, bottom], a3.at[c], gx_s.at[c, 1], gx_r.at[c, 1], at_x(3)),
        ]

        def body(j, carry):
            g = (3 + j) % NX
            down = wd[:, c * cc : (c + 1) * cc]
            p[c, g] = jnp.dot(act[g], down, preferred_element_type=F32).astype(BF16)
            return carry

        lax.fori_loop(0, 3, body, 0)

    def gather_x(c):
        gx[c][0].wait_recv()
        p[c, 1, 0:half] = (p[c, 1, 0:half].astype(F32) + a1[c].astype(F32)).astype(BF16)
        first = send(p.at[c, 1], bl.at[c], gx_s.at[c, 2], gx_r.at[c, 2], at_x(1))
        gx[c][1].wait_recv()
        p[c, 3, half:rows] = (p[c, 3, half:rows].astype(F32) + a3[c].astype(F32)).astype(BF16)
        second = send(p.at[c, 3], br.at[c], gx_s.at[c, 3], gx_r.at[c, 3], at_x(3))
        gw[c] = [first, second]

    def back_y(c):
        for copy in gw[c]:
            copy.wait_recv()
        total = p[c, 0].astype(F32) + bl[c].astype(F32) + br[c].astype(F32)
        total = total.astype(BF16).reshape(2 * NY, slots, cc)
        v[c, 0] = total[0]
        zz[c] = total
        gy[c] = [
            send(zz.at[c, d], v.at[c, flip_y(d)], gy_s.at[c, d], gy_r.at[c, flip_y(d)], at_y(d))
            for d in (1, 2, 6, 3, 7, 4, 5)
        ]

    def back_z(c):
        for copy in gy[c]:
            copy.wait_recv()
        part = jnp.dot(wt[...], v[c].reshape(rows, cc), preferred_element_type=F32)
        zsend[c] = part.astype(BF16).reshape(NZ, tree, cc)
        gz[c] = [
            send(zsend.at[c, k], zrecv.at[c, NZ - k], gz_s.at[c, k], gz_r.at[c, NZ - k], at_z(k))
            for k in (1, 7, 2, 6, 3, 5, 4)
        ]

    def finish(c):
        for copy in gz[c]:
            copy.wait_recv()
        total = mixed[c].astype(F32) + zsend[c, 0].astype(F32)
        for k in range(1, NZ):
            total = total + zrecv[c, k].astype(F32)
        out_ref[:, c * cc : (c + 1) * cc] = total.astype(BF16)

    for i in range(CHUNKS + 4):
        if i < CHUNKS:
            contract(i)
        if 0 <= i - 1 < CHUNKS:
            gather_x(i - 1)
        if 0 <= i - 2 < CHUNKS:
            back_y(i - 2)
        if 0 <= i - 3 < CHUNKS:
            back_z(i - 3)
        if 0 <= i - 4 < CHUNKS:
            finish(i - 4)

    for copy in started:
        copy.wait_send()


def run_layer(head_out, hidden, gain, table, out_proj, w_gate, w_up, w_down):
    tree, width = hidden.shape
    cc = width // CHUNKS
    hid = w_gate.shape[1]
    slots = table.shape[1]
    rows = NZ * slots
    cols = NZ * tree
    i = jnp.arange(rows, dtype=jnp.int32)
    cap = slots // (2 * NY)
    source = ((i % slots) // cap) * slots + (i // slots) * cap + i % cap
    perm = (source[:, None] == i[None, :]).astype(BF16)
    j = jnp.arange(2 * cols, dtype=jnp.int32)
    lane = jnp.arange(128, dtype=jnp.int32)
    spread = ((j[None, :] // cols) * tree + j[None, :] % tree == lane[:, None]).astype(BF16)
    mask = ((i[:, None] // slots) == ((j[None, :] % cols) // tree)).astype(BF16)
    vmem = pl.BlockSpec(memory_space=pltpu.VMEM)
    hbm = pl.BlockSpec(memory_space=pl.ANY)
    dma = pltpu.SemaphoreType.DMA
    c = CHUNKS
    return pl.pallas_call(
        layer_kernel,
        out_shape=jax.ShapeDtypeStruct((tree, width), BF16),
        in_specs=[vmem] * 7 + [hbm] * 4,
        out_specs=vmem,
        scratch_shapes=[
            pltpu.VMEM(out_proj.shape, BF16),
            pltpu.VMEM(w_gate.shape, BF16),
            pltpu.VMEM(w_up.shape, BF16),
            pltpu.VMEM(w_down.shape, BF16),
            pltpu.VMEM((NX, tree, width), BF16),
            pltpu.VMEM((NX, tree, width // NX), BF16),
            pltpu.VMEM((NX, tree, width // NX), BF16),
            pltpu.VMEM((c, tree, cc), BF16),
            pltpu.VMEM((NZ, slots, 128), BF16),
            pltpu.VMEM((rows, cols), BF16),
            pltpu.VMEM((cols, rows), BF16),
            pltpu.VMEM((c, NZ, tree, cc), BF16),
            pltpu.VMEM((c, 2 * NY, slots, cc), BF16),
            pltpu.VMEM((c, NX, rows, cc), BF16),
            pltpu.VMEM((NX, rows, hid), F32),
            pltpu.VMEM((NX, rows, hid), F32),
            pltpu.VMEM((NX, rows, hid), BF16),
            pltpu.VMEM((c, NX, rows, cc), BF16),
            pltpu.VMEM((c, rows // 2, cc), BF16),
            pltpu.VMEM((c, rows // 2, cc), BF16),
            pltpu.VMEM((c, rows, cc), BF16),
            pltpu.VMEM((c, rows, cc), BF16),
            pltpu.VMEM((c, 2 * NY, slots, cc), BF16),
            pltpu.VMEM((c, 2 * NY, slots, cc), BF16),
            pltpu.VMEM((c, NZ, tree, cc), BF16),
            pltpu.VMEM((c, NZ, tree, cc), BF16),
            dma((4,)),
            dma((NX,)), dma((NX,)), dma((NX,)), dma((NX,)),
            dma((NZ,)), dma((NZ,)),
            dma((c, NZ)), dma((c, NZ)), dma((c, 2 * NY)), dma((c, 2 * NY)),
            dma((c, 4)), dma((c, 4)), dma((c, 4)), dma((c, 4)),
            dma((c, 2 * NY)), dma((c, 2 * NY)), dma((c, NZ)), dma((c, NZ)),
        ],
        compiler_params=pltpu.CompilerParams(
            collective_id=0, has_side_effects=True, vmem_limit_bytes=60 * 1024 * 1024
        ),
        name="layer",
    )(head_out, hidden, gain, table, perm, spread, mask, out_proj, w_gate, w_up, w_down)


def local(
    hidden, queries, new_latent, pages, page_table, cache_len, parents, accept_path, accept_count,
    key_up, value_up, out_proj, norm_gain, route_ids, route_weights, w_gate, w_up, w_down,
):
    rx = lax.axis_index("req")
    e = lax.axis_index("exp")
    experts = lax.axis_size("exp") * w_gate.shape[0]
    capacity = max(2, min(TREE, 2 * TREE * TOP // experts))
    order = jnp.arange(experts, dtype=jnp.int32)
    expert_ids = (
        ((e // (2 * NY) + order // (2 * NY)) % NZ) * (2 * NY)
        + ((e // 2 + order // 2) % NY) * 2
        + (e + order) % 2
    )
    ids = lax.dynamic_index_in_dim(route_ids[:, 0], rx, 0, keepdims=False)
    wts = lax.dynamic_index_in_dim(route_weights[:, 0], rx, 0, keepdims=False)
    table = slot_table(ids, wts, expert_ids, capacity)
    head_out = attend(
        queries[0], pages, page_table[0], cache_len[0], parents[0], new_latent[0], key_up, value_up
    )
    layer_out = run_layer(
        head_out, hidden[0], norm_gain[None], table, out_proj, w_gate[0], w_up[0], w_down[0]
    )
    new_pool = write_rows(
        pages, page_table[0], cache_len[0], accept_path[0], accept_count[0], new_latent[0]
    )
    return (layer_out[None], new_pool)


def solution(mesh):
    in_specs = (
        P(("req", "exp"), None, None),
        P(("req", "exp"), None, None),
        P(("req", "exp"), None, None),
        P(("req", "exp"), None, None),
        P(("req", "exp"), None),
        P(("req", "exp")),
        P(("req", "exp"), None),
        P(("req", "exp"), None),
        P(("req", "exp")),
        P(),
        P(),
        P(None, "req"),
        P(),
        P(None, "exp", None, None),
        P(None, "exp", None, None),
        P("exp", None, "req"),
        P("exp", None, "req"),
        P("exp", "req", None),
    )
    out_specs = (P(("req", "exp"), None, None), P(("req", "exp"), None, None))
    return jax.shard_map(local, mesh=mesh, in_specs=in_specs, out_specs=out_specs, check_vma=False)
```

time: 503 us -> 223 us (0.44); the launches traced: 495 us -> 222 us
  blocking collectives: 182 us -> 0 us
  Pallas kernels: 0 us -> 168 us
  waiting for transfers between devices: 146 us -> 0 us
  local copies, waits for them, and re-layouts: 82.9 us -> 19.8 us
  matrix products: 45.8 us -> 12.9 us
  between operations: 16 us -> 2.21 us
  starting transfers between devices: 10.8 us -> 0 us
  other arithmetic: 11.5 us -> 18.8 us
    pallas_call x0 -> x1, Pallas kernels: none -> 168 us  [run_layer(): pl.pallas_call(layer_kernel, out_shape=jax.ShapeDtypeStruct((tree, width)...]
    all_to_all x1 -> x0, blocking collectives: 159 us -> none  [local(): lax.all_to_all(outbound, 'exp', split_axis=0, concat_axis=0, tiled=True)]
    all_to_all x2 -> x0, waiting for transfers between devices: 143 us -> none  [the longest x1 138 us: local(): lax.all_to_all(jnp.dot(active, down_local, preferred_element_type=jnp.flo...]
    reshape x3 -> x1, local copies, waits for them, and re-layouts: 41.3 us -> 1.56 us  [slot_table(): return both.reshape(NZ, -1, 128)]
    dot_general x9 -> x6, matrix products: 42.9 us -> 10.1 us  [the longest x1 3.38 us: attend(): jnp.einsum('thc,hcv->thv', context, value_up, preferred_element_type=F32)]
    all_gather x2 -> x0, blocking collectives: 22.5 us -> none  [the longest x1 12.3 us: local(): lax.all_gather(head_out, 'req', axis=0, tiled=True)]
    gather x3 -> x0, local copies, waits for them, and re-layouts: 12 us -> none  [the longest x1 6.56 us: write_rows(): source = jnp.take(path_row, jnp.clip(offset, 0, path_row.shape[0] - 1))]
    all_to_all x2 -> x0, starting transfers between devices: 10.8 us -> none  [the longest x1 7.35 us: local(): lax.all_to_all(jnp.dot(active, down_local, preferred_element_type=jnp.flo...]
  transfers between devices with their start and end apart: 3 -> 0, of which waited for: 3 -> 0; matrix products, arithmetic and copies ran while one was open for 3% -> 0% of each run, Pallas kernels for 0% -> 0%
where the time goes in v1:
time: 223 us; the launch traced here: 222 us
  Pallas kernels  168 us (75%)
  local copies, waits for them, and re-layouts  19.8 us (9%)
  other arithmetic  18.8 us (8%)
  matrix products  12.9 us (6%)
    pallas_call x1, Pallas kernels, run_layer(): pl.pallas_call(layer_kernel, out_shape=jax.ShapeDtypeStruct((tree, width)...  168 us
    unnamed x40, local copies, waits for them, and re-layouts  5.75 us

profile of v1, /device:TPU:1, one launch (start us, length us, event | category | flops | bytes accessed | tf_op | source)
XLA Modules:
  0.0 222.2 jit_solution(14047137314730695179)
XLA Ops:
  0.6 1.4 reshape_squeeze.3
  2.8 0.9 pad_maximum_fusion
  4.5 2.0 gather_fusion
  6.5 1.5 copy.127
  8.0 1.6 bitcast_select_fusion
  9.7 2.4 %fusion = (f32[32,16]{1,0:T(8,128)S(1)}, f32[32,16,1024]{2,1,0:T(8,128)}) fusion(pred[1024]{0:T(1024)(128)(4,1)S(1)} %iota_compare_fusion.18, bf16[1024,576]{1,0:T(8,128)(2,1)S(1)} %bitcast_select_fusion, bf16[32,16,576]{2,0,1:T(8,128)(2,1)S(1)} %copy-done.7), kind=kOutput, calls=%fused_computation.4 | convolution fusion | flops 605552128 | bytes 3869696 | tf_op jit(solution)/shard_map/thc,kc->thk/dot_general | solution.py:44
  13.4 1.4 fusion.99
  14.9 2.1 fusion.1
  17.2 1.1 fusion.22
  18.4 2.1 divide_convert_fusion
  20.5 1.8 fusion.12
  22.2 3.4 %fusion.10 = bf16[16,4,8,128]{3,2,1,0:T(8,128)(2,1)} fusion(bf16[16,512,128]{2,1,0:T(8,128)(2,1)} %param.28, f32[32,16,512]{2,0,1:T(8,128)} %fusion.12, f32[32,16,32]{0,2,1:T(8,128)} %get-tuple-element.5, f32[32,16]{0,1:T(8,128)S(1)} %add.231, f32[32,16]{0,1:T(8,128)S(1)} %max.7, bf16[32,576]{1,0:T(8,128)(2,1)} %bitcast.78), kind=kOutput, calls=%fused_computation.20 | convolution fusion | flops 84525056 | bytes 3575808 | tf_op jit(solution)/shard_map/thc,hcv->thv/dot_general | solution.py:58
  25.6 1.6 copy.148
  30.4 1.4 copy.119
  32.5 1.4 fusion.30
  33.9 1.4 copy.121
  36.6 0.9 select_convert_fusion
  39.1 1.6 reshape.340.tab_ref
  40.7 1.6 copy.122
  42.2 2.6 %copy.123 = bf16[1,2048,352]{2,1,0:T(8,128)(2,1)} copy(bf16[1,2048,352]{1,2,0:T(8,128)(2,1)} %param.34) | data formatting | bytes 2883584 | tf_op args[16]
  44.8 0.9 compare_convert_fusion.mask_ref
  47.9 168.5 %layer.1 = bf16[32,2048]{1,0:T(8,128)(2,1)} custom-call(bf16[32,2048]{1,0:T(8,128)(2,1)} %bitcast.76, bf16[32,2048]{1,0:T(8,128)(2,1)} %bitcast.79, bf16[1,2048]{1,0:T(2,128)(2,1)} %broadcast_in_dim.127.gain_ref, bf16[8,48,128]{2,1,0:T(8,128)(2,1)} %reshape.340.tab_ref, bf16[384,384]{1,0:T(8,128)(2,1)} %fusion.15.perm_ref, ...), custom_call_target="tpu_custom_call" | custom-call | tf_op jit(solution)/shard_map/layer/pallas_call | solution.py:362
  216.6 1.7 fusion.2
  219.0 2.5 %bitcast_select_fusion.1 = bf16[8,128,576]{1,2,0:T(8,128)(2,1)} fusion(bf16[8,128,576]{1,2,0:T(8,128)(2,1)S(1)} %copy-done.1, bf16[72,8,8,128]{3,2,1,0:T(8,128)(2,1)} %fusion.2, pred[8,128]{1,0:T(8,128)(4,1)S(1)} %fusion.68), kind=kLoop, calls=%fused_computation.16 | loop fusion | flops 589824 | bytes 3539968 | tf_op jit(solution)/shard_map/jit(_where)/select_n | solution.py:78
  (76 shorter events, 12.3 us)
Async XLA Ops:
  0.6 1.7 copy-start
  2.3 2.1 copy-start.15
  2.7 1.7 copy-start.2
  8.0 1.7 copy-start.7
  9.7 2.4 %copy-start.5 = (bf16[1024,576]{1,0:T(8,128)(2,1)}, bf16[1024,576]{1,0:T(8,128)(2,1)S(1)}, u32[]{:S(2)}) copy-start(bf16[1024,576]{1,0:T(8,128)(2,1)S(1)} %bitcast_select_fusion) | copy-start | bytes 3538948
  9.7 2.5 %copy-start.14 = (s32[1,32]{1,0:T(1,128)S(1)}, s32[1,32]{1,0:T(1,128)}, u32[]{:S(2)}) copy-start(s32[1,32]{1,0:T(1,128)} %param.24) | copy-start | bytes 388
  9.7 3.7 %copy-start.3 = (bf16[32,16,512]{2,0,1:T(8,128)(2,1)S(1)}, bf16[32,16,512]{2,0,1:T(8,128)(2,1)}, u32[]{:S(2)}) copy-start(bf16[32,16,512]{2,0,1:T(8,128)(2,1)} %copy-done.2) | copy-start | bytes 1572868
  9.7 3.7 %copy-start.9 = (bf16[1,32,576]{2,1,0:T(8,128)(2,1)S(1)}, bf16[1,32,576]{2,1,0:T(8,128)(2,1)}, u32[]{:S(2)}) copy-start(bf16[1,32,576]{2,1,0:T(8,128)(2,1)} %param.20) | copy-start | bytes 110596
  17.1 3.4 %copy-start.6 = (bf16[1024,576]{1,0:T(8,128)(2,1)S(1)}, bf16[1024,576]{1,0:T(8,128)(2,1)}, u32[]{:S(2)}) copy-start(bf16[1024,576]{1,0:T(8,128)(2,1)} %copy-done.5) | copy-start | bytes 3538948
  22.2 18.4 %copy-start.4 = (bf16[1,2048,352]{1,2,0:T(8,128)(2,1)S(1)}, bf16[1,2048,352]{1,2,0:T(8,128)(2,1)}, u32[]{:S(2)}) copy-start(bf16[1,2048,352]{1,2,0:T(8,128)(2,1)} %param.33) | copy-start | bytes 4325380
  28.4 0.6 copy-start.11
  42.2 5.0 %copy-start.12 = (bf16[2048]{0:T(1024)(128)(2,1)S(1)}, bf16[2048]{0:T(1024)(128)(2,1)}, u32[]{:S(2)}) copy-start(bf16[2048]{0:T(1024)(128)(2,1)} %param.30) | copy-start | bytes 12292
  47.9 168.5 %copy-start.16 = (s32[1,8]{1,0:T(1,128)S(1)}, s32[1,8]{1,0:T(1,128)}, u32[]{:S(2)}) copy-start(s32[1,8]{1,0:T(1,128)} %param.22) | copy-start | bytes 100
  47.9 168.7 %copy-start.10 = (bf16[1,32,576]{2,1,0:T(8,128)(2,1)S(1)}, bf16[1,32,576]{2,1,0:T(8,128)(2,1)}, u32[]{:S(2)}) copy-start(bf16[1,32,576]{2,1,0:T(8,128)(2,1)} %param.20) | copy-start | bytes 110596
  47.9 168.7 %copy-start.13 = (s32[1,32]{1,0:T(1,128)S(1)}, s32[1,32]{1,0:T(1,128)}, u32[]{:S(2)}) copy-start(s32[1,32]{1,0:T(1,128)} %param.25) | copy-start | bytes 388
  47.9 171.2 %copy-start.1 = (bf16[8,128,576]{1,2,0:T(8,128)(2,1)S(1)}, bf16[8,128,576]{1,2,0:T(8,128)(2,1)}, u32[]{:S(2)}) copy-start(bf16[8,128,576]{1,2,0:T(8,128)(2,1)} %param.21) | copy-start | bytes 3538948
  216.6 5.0 %copy-start.8 = (bf16[32,2048]{1,0:T(8,128)(2,1)S(1)}, bf16[32,2048]{1,0:T(8,128)(2,1)}, u32[]{:S(2)}) copy-start(bf16[32,2048]{1,0:T(8,128)(2,1)} %layer.1) | copy-start | bytes 393220

commit v2 on v1

v2 whole, which is shorter than its diff:
```python
import math

import jax
import jax.numpy as jnp
import numpy as np
from jax import lax
from jax.experimental import pallas as pl
from jax.experimental.pallas import tpu as pltpu
from jax.sharding import PartitionSpec as P

MESH = pl.DeviceIdType.MESH
NX = 4
NY = 4
NZ = 8
CHUNKS = 8
F32 = jnp.float32
BF16 = jnp.bfloat16


def dot(a, b, contract=((1,), (0,))):
    return lax.dot_general(a, b, (contract, ((), ())), preferred_element_type=F32)


def build_table(tab, ids, weights, rep_ref, slot_ref, ez, ey, ec):
    top, tree = ids.shape
    n = NZ * NY * 2
    order = lax.broadcasted_iota(jnp.int32, (n, 1), 0)
    expert = (
        ((ez + (order >> 3)) & 7) * 8 + ((ey + ((order >> 1) & 3)) & 3) * 2 + ((ec + order) & 1)
    )
    chosen = jnp.zeros((n, tree), F32)
    weight = jnp.zeros((n, tree), F32)
    for k in range(top):
        hit = ids[k : k + 1, :] == expert
        chosen = chosen + jnp.where(hit, 1.0, 0.0)
        weight = weight + jnp.where(hit, weights[k : k + 1, :], 0.0)
    one = lax.broadcasted_iota(jnp.int32, (tree, tree), 0)
    two = lax.broadcasted_iota(jnp.int32, (tree, tree), 1)
    earlier = jnp.where(one < two, 1.0, 0.0).astype(BF16)
    before = dot(chosen.astype(BF16), earlier)
    rep = rep_ref[...]
    taken = dot(rep, chosen.astype(BF16))
    rank = dot(rep, before.astype(BF16))
    amount = dot(rep, weight.astype(BF16))
    placed = jnp.logical_and(taken > 0.5, rank == slot_ref[...])
    tab[...] = jnp.zeros(tab.shape, BF16)
    shape = (tab.shape[0], tab.shape[1], tree)
    tab[:, :, 0:tree] = jnp.where(placed, 1.0, 0.0).astype(BF16).reshape(shape)
    tab[:, :, tree : 2 * tree] = jnp.where(placed, amount, 0.0).astype(BF16).reshape(shape)


def ancestors(parents, tree):
    one = lax.broadcasted_iota(jnp.int32, (tree, tree), 0)
    two = lax.broadcasted_iota(jnp.int32, (tree, tree), 1)
    reach = jnp.where(jnp.logical_or(one == parents, one == two), 1.0, 0.0)
    for sweep in range((tree - 1).bit_length()):
        half = reach.astype(BF16)
        reach = jnp.minimum(dot(half, half), 1.0)
    return reach.T


def attend(q_ref, fresh_ref, kt, ku, vu, qs, ctx, heads, live, reach, ku_in, kt_in, vu_in):
    n_heads, nope, latent = ku.shape
    tree = q_ref.shape[0]
    per = q_ref.shape[1] // n_heads
    scale = 1.0 / math.sqrt(per)
    ku_in.wait()
    for h in range(n_heads):
        rows = pl.ds(h * tree, tree)
        q_nope = q_ref[:, h * per : h * per + nope]
        qs[rows, 0:latent] = dot(q_nope, ku[h]).astype(BF16)
        qs[rows, latent:] = q_ref[:, h * per + nope : (h + 1) * per]
    kt_in.wait()
    block = 128
    pairs = kt.shape[0] // 2
    page = kt.shape[2]
    fresh = fresh_ref[...]
    allowed = jnp.concatenate([reach] * (block // tree), axis=0) > 0.5

    def body(i, carry):
        at = pl.multiple_of(i * block, block)
        q = qs[pl.ds(at, block), :]
        tree_score = jnp.where(allowed, dot(q, fresh, ((1,), (1,))) * scale, -1e30)
        scores = []
        for j in range(pairs):
            keys = jnp.concatenate([kt[2 * j], kt[2 * j + 1]], axis=1)
            mask = live[:, 2 * j * page : 2 * (j + 1) * page]
            scores.append(jnp.where(mask, dot(q, keys) * scale, -1e30))
        peak = jnp.max(tree_score, axis=1, keepdims=True)
        for s in scores:
            peak = jnp.maximum(peak, jnp.max(s, axis=1, keepdims=True))
        tree_score = jnp.exp(tree_score - peak)
        scores = [jnp.exp(s - peak) for s in scores]
        total = jnp.sum(tree_score, axis=1, keepdims=True)
        for s in scores:
            total = total + jnp.sum(s, axis=1, keepdims=True)
        inverse = 1.0 / total
        context = dot((tree_score * inverse).astype(BF16), fresh[:, 0:latent])
        for j in range(pairs):
            keys = jnp.concatenate([kt[2 * j, 0:latent], kt[2 * j + 1, 0:latent]], axis=1)
            context = context + dot((scores[j] * inverse).astype(BF16), keys, ((1,), (1,)))
        ctx[pl.ds(at, block), :] = context.astype(BF16)
        return carry

    lax.fori_loop(0, n_heads * tree // block, body, 0)
    vu_in.wait()
    for h in range(n_heads):
        out = dot(ctx[pl.ds(h * tree, tree), :], vu[h])
        heads[0, :, h * vu.shape[2] : (h + 1) * vu.shape[2]] = out.astype(BF16)


def write_pages(kt, fresh_ref, path, offset, count):
    steps = fresh_ref.shape[0]
    step = lax.broadcasted_iota(jnp.int32, (steps, 1), 0)
    by_step = jnp.where(step == path, 1.0, 0.0).astype(BF16)
    page = kt.shape[2]
    for j in range(kt.shape[0]):
        here = offset[:, j * page : (j + 1) * page]
        at_step = jnp.where(step == here, 1.0, 0.0).astype(BF16)
        pick = dot(by_step, at_step).astype(BF16)
        rows = dot(fresh_ref[...], pick, ((0,), (0,))).astype(BF16)
        valid = jnp.where(jnp.logical_and(here >= 0, here < count), 1.0, 0.0)
        old = kt[j]
        kt[j] = jnp.where(jnp.broadcast_to(valid, old.shape) > 0.5, rows.astype(F32), old.astype(F32)).astype(BF16)


def layer_kernel(
    ptab_ref, clen_ref, count_ref,
    hid_ref, q_ref, fresh_ref, parent_ref, path_ref, gain_ref, ids_ref, rw_ref,
    rep_ref, slot_ref, perm_ref, spread_ref, mask_ref,
    pages_hbm, ku_hbm, vu_hbm, oproj_hbm, wg_hbm, wu_hbm, wd_hbm,
    out_ref, newp_hbm,
    kt, ku, vu, qs, ctx,
    oproj, wg, wu, wd, heads, po, co, mixed, tab, tabs, sel, wt, tok, ysend, x, accg, accu, act,
    p, a1, a3, bl, br, zz, v, zsend, zrecv,
    w_sem, h_s, h_r, o_s, o_r, t_s, t_r, fz_s, fz_r, fy_s, fy_r, fx_s, fx_r,
    gx_s, gx_r, gy_s, gy_r, gz_s, gz_r,
):
    rx = lax.axis_index("req")
    e = lax.axis_index("exp")
    ez = e // (2 * NY)
    ey = (e // 2) % NY
    ec = e % 2
    width = hid_ref.shape[1]
    cc = width // CHUNKS
    slots = ysend.shape[2]
    rows = x.shape[2]
    half = rows // 2
    tree = hid_ref.shape[0]

    def at_x(k):
        return ((rx + k) % NX, e)

    def at_z(k):
        return (rx, (((ez + k) % NZ) * NY + ey) * 2 + ec)

    def at_y(d):
        return (rx, (ez * NY + (ey + d // 2) % NY) * 2 + (ec + d % 2) % 2)

    def flip_y(d):
        return ((NY - d // 2) % NY) * 2 + d % 2

    in_copies = [
        pltpu.make_async_copy(src, dst, w_sem.at[n])
        for n, (src, dst) in enumerate(
            [(ku_hbm, ku), (pages_hbm, kt), (vu_hbm, vu), (oproj_hbm, oproj), (wg_hbm, wg), (wu_hbm, wu), (wd_hbm, wd)]
        )
    ]
    ku_in, kt_in, vu_in, oproj_in, wg_in, wu_in, wd_in = in_copies
    for copy in in_copies:
        copy.start()

    barrier = pltpu.get_barrier_semaphore()
    partners = (
        [at_x(k) for k in range(1, NX)]
        + [at_y(d) for d in range(1, 2 * NY)]
        + [at_z(k) for k in range(1, NZ)]
    )
    for partner in partners:
        pl.semaphore_signal(barrier, inc=1, device_id=partner, device_id_type=MESH)

    build_table(tab, ids_ref[rx], rw_ref[rx], rep_ref, slot_ref, ez, ey, ec)
    page_len = kt.shape[2]
    n_pages = kt.shape[0]
    lane = lax.broadcasted_iota(jnp.int32, (1, page_len), 1)
    position = []
    for j in range(n_pages):
        logical = jnp.int32(0)
        for k in range(n_pages):
            logical = logical + jnp.where(ptab_ref[0, k] == j, k, 0)
        position.append(logical * page_len + lane)
    position = jnp.concatenate(position, axis=1)
    length = clen_ref[0]
    reach = ancestors(parent_ref[...], tree)

    pl.semaphore_wait(barrier, len(partners))

    started = []

    def send(src, dst, ss, rs, device):
        copy = pltpu.make_async_remote_copy(
            src_ref=src, dst_ref=dst, send_sem=ss, recv_sem=rs, device_id=device, device_id_type=MESH
        )
        copy.start()
        started.append(copy)
        return copy

    tabs[0] = tab[0]
    tab_copies = [send(tab.at[k], tabs.at[NZ - k], t_s.at[k], t_r.at[NZ - k], at_z(k)) for k in range(1, NZ)]

    attend(q_ref, fresh_ref, kt, ku, vu, qs, ctx, heads, position < length, reach, ku_in, kt_in, vu_in)
    head_copies = [
        send(heads.at[0], heads.at[NX - k], h_s.at[k], h_r.at[NX - k], at_x(k)) for k in (1, 3, 2)
    ]
    for copy in tab_copies:
        copy.wait_recv()
    flat_tabs = tabs[...].reshape(NZ * slots, 128)
    wide = dot(flat_tabs, spread_ref[...]) * mask_ref[...].astype(F32)
    both = dot(perm_ref[...], wide.astype(BF16))
    sel[...] = both[:, : NZ * tree].astype(BF16)
    wt[...] = both[:, NZ * tree :].T.astype(BF16)

    oproj_in.wait()
    for copy in head_copies:
        copy.wait_recv()
    proj = jnp.dot(heads[...].reshape(NX * tree, width), oproj[...], preferred_element_type=F32)
    po[...] = proj.astype(BF16).reshape(po.shape)
    back_copies = [send(po.at[k], co.at[rx], o_s.at[k], o_r.at[NX - k], at_x(k)) for k in (1, 3, 2)]
    co[rx] = po[0]
    for copy in back_copies:
        copy.wait_recv()
    square = jnp.zeros((tree, 1), F32)
    for c in range(CHUNKS):
        per = width // NX
        at = c * cc % per
        column = co[c * cc // per, :, at : at + cc].astype(F32)
        m = (hid_ref[:, c * cc : (c + 1) * cc].astype(F32) + column).astype(BF16)
        mixed[c] = m
        mf = m.astype(F32)
        square = square + jnp.sum(mf * mf, axis=1, keepdims=True)
    factor = lax.rsqrt(square * (1.0 / width) + 1e-06)

    fz, fy, fx, fw = {}, {}, {}, {}
    for c in range(CHUNKS):
        gain = gain_ref[:, c * cc : (c + 1) * cc].astype(F32)
        tok[c, 0] = (mixed[c].astype(F32) * factor * gain).astype(BF16)
        fz[c] = [
            send(tok.at[c, 0], tok.at[c, NZ - k], fz_s.at[c, k], fz_r.at[c, NZ - k], at_z(k))
            for k in (1, 7, 2, 6, 3, 5, 4)
        ]

    def select(c):
        for copy in fz[c]:
            copy.wait_recv()
        block = jnp.dot(sel[...], tok[c].reshape(NZ * tree, cc), preferred_element_type=F32)
        block = block.astype(BF16)
        x[c, 0, 0:slots] = block[0:slots]
        ysend[c] = block.reshape(2 * NY, slots, cc)
        fy[c] = [
            send(
                ysend.at[c, d],
                x.at[c, 0, pl.ds(flip_y(d) * slots, slots)],
                fy_s.at[c, d],
                fy_r.at[c, flip_y(d)],
                at_y(d),
            )
            for d in (1, 2, 6, 3, 7, 4, 5)
        ]

    def spread_x(c):
        for copy in fy[c]:
            copy.wait_recv()
        fx[c] = [
            send(x.at[c, 0], x.at[c, 3], fx_s.at[c, 0], fx_r.at[c, 0], at_x(1)),
            send(x.at[c, 0], x.at[c, 1], fx_s.at[c, 1], fx_r.at[c, 1], at_x(3)),
        ]

    def forward_x(c):
        top, bottom = pl.ds(0, half), pl.ds(half, half)
        fx[c][0].wait_recv()
        first = send(x.at[c, 3, top], x.at[c, 2, top], fx_s.at[c, 2], fx_r.at[c, 2], at_x(1))
        fx[c][1].wait_recv()
        second = send(x.at[c, 1, bottom], x.at[c, 2, bottom], fx_s.at[c, 3], fx_r.at[c, 3], at_x(3))
        fw[c] = [first, second]

    def expand(c):
        for copy in fw[c]:
            copy.wait_recv()
        if c == 0:
            wg_in.wait()
            wu_in.wait()

        def body(g, carry):
            block = x[c, g]
            gv = dot(block, wg[:, c * cc : (c + 1) * cc], ((1,), (1,)))
            uv = dot(block, wu[:, c * cc : (c + 1) * cc], ((1,), (1,)))
            if c > 0:
                gv = gv + accg[g]
                uv = uv + accu[g]
            if c == CHUNKS - 1:
                act[g] = (gv * jax.nn.sigmoid(gv) * uv).astype(BF16)
            else:
                accg[g] = gv
                accu[g] = uv
            return carry

        lax.fori_loop(0, NX, body, 0)

    for i in range(CHUNKS + 3):
        if i < CHUNKS:
            select(i)
        if 0 <= i - 1 < CHUNKS:
            spread_x(i - 1)
        if 0 <= i - 2 < CHUNKS:
            forward_x(i - 2)
        if 0 <= i - 3 < CHUNKS:
            expand(i - 3)
        if i == 2:
            write_pages(kt, fresh_ref, path_ref[...], position - length, count_ref[0])
            page_out = pltpu.make_async_copy(kt, newp_hbm, w_sem.at[7])
            page_out.start()

    wd_in.wait()
    gx, gw, gy, gz = {}, {}, {}, {}

    def contract(c):
        top, bottom = pl.ds(0, half), pl.ds(half, half)
        down = wd[:, c * cc : (c + 1) * cc]
        p[c, 2] = jnp.dot(act[2], down, preferred_element_type=F32).astype(BF16)
        gx[c] = [
            send(p.at[c, 2, top], a1.at[c], gx_s.at[c, 0], gx_r.at[c, 0], at_x(1)),
            send(p.at[c, 2, bottom], a3.at[c], gx_s.at[c, 1], gx_r.at[c, 1], at_x(3)),
        ]

        def body(j, carry):
            g = (3 + j) % NX
            down = wd[:, c * cc : (c + 1) * cc]
            p[c, g] = jnp.dot(act[g], down, preferred_element_type=F32).astype(BF16)
            return carry

        lax.fori_loop(0, 3, body, 0)

    def gather_x(c):
        gx[c][0].wait_recv()
        p[c, 1, 0:half] = (p[c, 1, 0:half].astype(F32) + a1[c].astype(F32)).astype(BF16)
        first = send(p.at[c, 1], bl.at[c], gx_s.at[c, 2], gx_r.at[c, 2], at_x(1))
        gx[c][1].wait_recv()
        p[c, 3, half:rows] = (p[c, 3, half:rows].astype(F32) + a3[c].astype(F32)).astype(BF16)
        second = send(p.at[c, 3], br.at[c], gx_s.at[c, 3], gx_r.at[c, 3], at_x(3))
        gw[c] = [first, second]

    def back_y(c):
        for copy in gw[c]:
            copy.wait_recv()
        total = p[c, 0].astype(F32) + bl[c].astype(F32) + br[c].astype(F32)
        total = total.astype(BF16).reshape(2 * NY, slots, cc)
        v[c, 0] = total[0]
        zz[c] = total
        gy[c] = [
            send(zz.at[c, d], v.at[c, flip_y(d)], gy_s.at[c, d], gy_r.at[c, flip_y(d)], at_y(d))
            for d in (1, 2, 6, 3, 7, 4, 5)
        ]

    def back_z(c):
        for copy in gy[c]:
            copy.wait_recv()
        part = jnp.dot(wt[...], v[c].reshape(rows, cc), preferred_element_type=F32)
        zsend[c] = part.astype(BF16).reshape(NZ, tree, cc)
        gz[c] = [
            send(zsend.at[c, k], zrecv.at[c, NZ - k], gz_s.at[c, k], gz_r.at[c, NZ - k], at_z(k))
            for k in (1, 7, 2, 6, 3, 5, 4)
        ]

    def finish(c):
        for copy in gz[c]:
            copy.wait_recv()
        total = mixed[c].astype(F32) + zsend[c, 0].astype(F32)
        for k in range(1, NZ):
            total = total + zrecv[c, k].astype(F32)
        out_ref[:, c * cc : (c + 1) * cc] = total.astype(BF16)

    for i in range(CHUNKS + 4):
        if i < CHUNKS:
            contract(i)
        if 0 <= i - 1 < CHUNKS:
            gather_x(i - 1)
        if 0 <= i - 2 < CHUNKS:
            back_y(i - 2)
        if 0 <= i - 3 < CHUNKS:
            back_z(i - 3)
        if 0 <= i - 4 < CHUNKS:
            finish(i - 4)

    for copy in started:
        copy.wait_send()
    page_out.wait()


def constants(tree, cap):
    slots = 2 * NY * cap
    rows, cols = NZ * slots, NZ * tree
    i = np.arange(rows)
    source = ((i % slots) // cap) * slots + (i // slots) * cap + i % cap
    perm = source[:, None] == i[None, :]
    j = np.arange(2 * cols)
    lane = np.arange(128)
    spread = (j[None, :] // cols) * tree + j[None, :] % tree == lane[:, None]
    mask = (i[:, None] // slots) == ((j[None, :] % cols) // tree)
    rep = i[:, None] // cap == np.arange(rows // cap)[None, :]
    slot = (i % cap)[:, None].astype(np.float32)
    return [rep.astype(BF16), slot, perm.astype(BF16), spread.astype(BF16), mask.astype(BF16)]


def run_layer(
    hidden, queries, fresh, pages_t, page_table, cache_len, parents, accept_path, accept_count,
    key_up, value_up, out_proj, gain, ids, weights, wg_t, wu_t, w_down,
):
    tree, width = hidden.shape
    cc = width // CHUNKS
    hid = w_down.shape[0]
    n_heads = key_up.shape[0]
    cap = max(2, min(tree, 2 * tree * ids.shape[1] // (NZ * NY * 2)))
    slots = 2 * NY * cap
    rows = NZ * slots
    cols = NZ * tree
    smem = pl.BlockSpec(memory_space=pltpu.SMEM)
    vmem = pl.BlockSpec(memory_space=pltpu.VMEM)
    hbm = pl.BlockSpec(memory_space=pl.ANY)
    dma = pltpu.SemaphoreType.DMA
    c = CHUNKS
    return pl.pallas_call(
        layer_kernel,
        out_shape=(jax.ShapeDtypeStruct((tree, width), BF16), jax.ShapeDtypeStruct(pages_t.shape, BF16)),
        in_specs=[smem] * 3 + [vmem] * 13 + [hbm] * 7,
        out_specs=(vmem, hbm),
        scratch_shapes=[
            pltpu.VMEM(pages_t.shape, BF16),
            pltpu.VMEM(key_up.shape, BF16),
            pltpu.VMEM(value_up.shape, BF16),
            pltpu.VMEM((n_heads * tree, fresh.shape[1]), BF16),
            pltpu.VMEM((n_heads * tree, key_up.shape[2]), BF16),
            pltpu.VMEM(out_proj.shape, BF16),
            pltpu.VMEM(wg_t.shape, BF16),
            pltpu.VMEM(wu_t.shape, BF16),
            pltpu.VMEM(w_down.shape, BF16),
            pltpu.VMEM((NX, tree, width), BF16),
            pltpu.VMEM((NX, tree, width // NX), BF16),
            pltpu.VMEM((NX, tree, width // NX), BF16),
            pltpu.VMEM((c, tree, cc), BF16),
            pltpu.VMEM((NZ, slots, 128), BF16),
            pltpu.VMEM((NZ, slots, 128), BF16),
            pltpu.VMEM((rows, cols), BF16),
            pltpu.VMEM((cols, rows), BF16),
            pltpu.VMEM((c, NZ, tree, cc), BF16),
            pltpu.VMEM((c, 2 * NY, slots, cc), BF16),
            pltpu.VMEM((c, NX, rows, cc), BF16),
            pltpu.VMEM((NX, rows, hid), F32),
            pltpu.VMEM((NX, rows, hid), F32),
            pltpu.VMEM((NX, rows, hid), BF16),
            pltpu.VMEM((c, NX, rows, cc), BF16),
            pltpu.VMEM((c, rows // 2, cc), BF16),
            pltpu.VMEM((c, rows // 2, cc), BF16),
            pltpu.VMEM((c, rows, cc), BF16),
            pltpu.VMEM((c, rows, cc), BF16),
            pltpu.VMEM((c, 2 * NY, slots, cc), BF16),
            pltpu.VMEM((c, 2 * NY, slots, cc), BF16),
            pltpu.VMEM((c, NZ, tree, cc), BF16),
            pltpu.VMEM((c, NZ, tree, cc), BF16),
            dma((8,)),
            dma((NX,)), dma((NX,)), dma((NX,)), dma((NX,)),
            dma((NZ,)), dma((NZ,)),
            dma((c, NZ)), dma((c, NZ)), dma((c, 2 * NY)), dma((c, 2 * NY)),
            dma((c, 4)), dma((c, 4)), dma((c, 4)), dma((c, 4)),
            dma((c, 2 * NY)), dma((c, 2 * NY)), dma((c, NZ)), dma((c, NZ)),
        ],
        compiler_params=pltpu.CompilerParams(
            collective_id=0, has_side_effects=True, vmem_limit_bytes=60 * 1024 * 1024
        ),
        name="layer",
    )(
        page_table, cache_len, accept_count,
        hidden, queries, fresh, parents, accept_path, gain, ids, weights,
        *[jnp.asarray(value) for value in constants(tree, cap)],
        pages_t, key_up, value_up, out_proj, wg_t, wu_t, w_down,
    )


def local(
    hidden, queries, new_latent, pages, page_table, cache_len, parents, accept_path, accept_count,
    key_up, value_up, out_proj, norm_gain, route_ids, route_weights, w_gate, w_up, w_down,
):
    layer_out, pages_out = run_layer(
        hidden[0], queries[0], new_latent[0], jnp.swapaxes(pages, 1, 2), page_table, cache_len, parents,
        accept_path, accept_count, key_up, value_up, out_proj, norm_gain[None],
        jnp.swapaxes(route_ids[:, 0], 1, 2), jnp.swapaxes(route_weights[:, 0], 1, 2),
        jnp.swapaxes(w_gate[0], 0, 1), jnp.swapaxes(w_up[0], 0, 1), w_down[0],
    )
    return (layer_out[None], jnp.swapaxes(pages_out, 1, 2))


def solution(mesh):
    in_specs = (
        P(("req", "exp"), None, None),
        P(("req", "exp"), None, None),
        P(("req", "exp"), None, None),
        P(("req", "exp"), None, None),
        P(("req", "exp"), None),
        P(("req", "exp")),
        P(("req", "exp"), None),
        P(("req", "exp"), None),
        P(("req", "exp")),
        P(),
        P(),
        P(None, "req"),
        P(),
        P(None, "exp", None, None),
        P(None, "exp", None, None),
        P("exp", None, "req"),
        P("exp", None, "req"),
        P("exp", "req", None),
    )
    out_specs = (P(("req", "exp"), None, None), P(("req", "exp"), None, None))
    return jax.shard_map(local, mesh=mesh, in_specs=in_specs, out_specs=out_specs, check_vma=False)
```

time: 223 us -> 177 us (0.79)
  other arithmetic: 18.8 us -> 0 us
  matrix products: 12.9 us -> 0 us
  local copies, waits for them, and re-layouts: 19.8 us -> 7.86 us
    dot_general x10 -> x0, matrix products: 12.9 us -> none  [the longest x1 3.38 us: attend(): jnp.einsum('thc,hcv->thv', context, value_up, preferred_element_type=F32)]
    convert_element_type x6 -> x0, other arithmetic: 6.2 us -> none  [the longest x1 2.11 us: attend(): prob_cache = (exp_cache / total).astype(BF16)]
    reduce_sum x5 -> x0, other arithmetic: 5.41 us -> none  [the longest x1 2.13 us: attend(): jnp.sum(exp_cache, axis=2, keepdims=True)]
    select_n x5 -> x0, other arithmetic: 4.17 us -> none  [the longest x1 2.54 us: write_rows(): jnp.where(valid[:, :, None], written.reshape(page_pool.shape), page_pool)]
    gather x2 -> x0, local copies, waits for them, and re-layouts: 3.5 us -> none  [attend(): jnp.take(page_pool, table_row, axis=0).reshape(-1, page_pool.shape[2])]
    reshape x2 -> x0, local copies, waits for them, and re-layouts: 3.15 us -> none  [the longest x1 1.59 us: attend(): return head_out.reshape(count, -1)]
    unnamed x40 -> x4, local copies, waits for them, and re-layouts: 5.75 us -> 5.36 us
where the time goes in v2:
time: 177 us
  Pallas kernels  167 us (94%)
  local copies, waits for them, and re-layouts  7.86 us (4%)
  between operations  1.93 us (1%)
    pallas_call x1, Pallas kernels, run_layer(): pl.pallas_call(layer_kernel, out_shape=(jax.ShapeDtypeStruct((tree, width...  167 us
    unnamed x4, local copies, waits for them, and re-layouts  5.36 us

profile of v2, /device:TPU:1, one launch (start us, length us, event | category | flops | bytes accessed | tf_op | source)
XLA Modules:
  0.0 177.0 jit_solution(8154979727351698398)
XLA Ops:
  1.9 1.3 broadcast_in_dim.6.gain_ref
  3.2 0.7 copy.36
  3.9 0.6 copy.34
  4.5 0.7 copy.35
  5.2 0.6 copy.33
  5.8 167.2 %layer.1 = (bf16[32,2048]{1,0:T(8,128)(2,1)}, bf16[8,576,128]{2,1,0:T(8,128)(2,1)}) custom-call(s32[1,8]{1,0:T(1,128)} %ptab_ref.1, s32[1]{0:T(128)S(6)} %copy.39.clen_ref, s32[1]{0:T(128)S(6)} %copy.40.count_ref, bf16[32,2048]{1,0:T(8,128)(2,1)} %bitcast.31, bf16[32,3072]{1,0:T(8,128)(2,1)} %bitcast.30, bf16[32,576]{1,0:T(8,128)(2,1)} %bitcast.37, ...), custom_call_target="tpu_custom_call" | custom-call | tf_op jit(solution)/shard_map/layer/pallas_call | solution.py:431
  173.0 1.6 copy.41
  174.6 2.4 %copy.42 = bf16[8,128,576]{1,2,0:T(8,128)(2,1)} copy(bf16[8,128,576]{1,2,0:T(8,128)(2,1)} %bitcast.28) | data formatting | bytes 2359296

commit v3 on v2

v3 whole, which is shorter than its diff:
```python
import math

import jax
import jax.numpy as jnp
import numpy as np
from jax import lax
from jax.experimental import pallas as pl
from jax.experimental.pallas import tpu as pltpu
from jax.sharding import PartitionSpec as P

MESH = pl.DeviceIdType.MESH
NX = 4
NY = 4
NZ = 8
CHUNKS = 8
EARLY = 2
LATE = CHUNKS - EARLY
EARLY_Z_AT = (0, 1)
EARLY_RELAY_AT = (2, 3)
SELECT_AT = (4, 5)
EXPAND_AT = (6, 8)
CONTRACT_AT = (0, 1)
BACK_Z_AT = (2, 4)
BACK_RELAY_AT = (3, 5)
BACK_X_AT = (5, 7)
F32 = jnp.float32
BF16 = jnp.bfloat16


def dot(a, b, contract=((1,), (0,))):
    return lax.dot_general(a, b, (contract, ((), ())), preferred_element_type=F32)


def pack_routes(ids_ref, weights_ref, rx):
    top, tree = ids_ref.shape[1], ids_ref.shape[3]
    ids = jnp.concatenate([ids_ref[rx, k].astype(F32) for k in range(top)], axis=0)
    weights = jnp.concatenate([weights_ref[rx, k] for k in range(top)], axis=0)
    both = jnp.concatenate([ids, weights, jnp.zeros((top, 128 - 2 * tree), F32)], axis=1)
    return jnp.concatenate([both, jnp.zeros((16 - top, 128), F32)], axis=0).astype(BF16)


def selection(routes, g, top, tree, const_ref, ez, ey, ec):
    n = routes.shape[0]
    tiles = [routes[k, g].astype(F32) for k in range(n)]
    ids = jnp.concatenate([t[0:top, 0:tree] for t in tiles], axis=1)
    weights = jnp.concatenate([t[0:top, tree : 2 * tree] for t in tiles], axis=1)
    order = lax.broadcasted_iota(jnp.int32, (2 * NY, 1), 0)
    expert = (ez * (2 * NY) + ((ey + (order >> 1)) & 3) * 2 + ((ec + order) & 1)).astype(F32)
    cols = n * tree
    chosen = jnp.zeros((2 * NY, cols), F32)
    weight = jnp.zeros((2 * NY, cols), F32)
    for k in range(top):
        hit = ids[k : k + 1, :] == expert
        chosen = chosen + jnp.where(hit, 1.0, 0.0)
        weight = weight + jnp.where(hit, weights[k : k + 1, :], 0.0)
    one = lax.broadcasted_iota(jnp.int32, (cols, cols), 0)
    two = lax.broadcasted_iota(jnp.int32, (cols, cols), 1)
    earlier = jnp.logical_and((one >> 5) == (two >> 5), one < two)
    before = dot(chosen.astype(BF16), jnp.where(earlier, 1.0, 0.0).astype(BF16))
    which = lax.broadcasted_iota(jnp.int32, (1, 2 * NY), 1)
    copy_rows = jnp.where(const_ref[:, 0:1] == which, 1.0, 0.0).astype(BF16)
    lane = lax.broadcasted_iota(jnp.int32, (1, cols), 1)
    taken = dot(copy_rows, chosen.astype(BF16))
    rank = dot(copy_rows, before.astype(BF16))
    amount = dot(copy_rows, weight.astype(BF16))
    placed = jnp.logical_and(taken > 0.5, rank == const_ref[:, 2:3].astype(F32))
    placed = jnp.logical_and(placed, const_ref[:, 1:2] == (lane >> 5))
    return jnp.where(placed, 1.0, 0.0).astype(BF16), jnp.where(placed, amount, 0.0).T.astype(BF16)


def ancestors(parents, tree):
    one = lax.broadcasted_iota(jnp.int32, (tree, tree), 0)
    two = lax.broadcasted_iota(jnp.int32, (tree, tree), 1)
    reach = jnp.where(jnp.logical_or(one == parents, one == two), 1.0, 0.0)
    for sweep in range((tree - 1).bit_length()):
        half = reach.astype(BF16)
        reach = jnp.minimum(dot(half, half), 1.0)
    return reach.T


def make_queries(q_ref, ku, qs, arriving):
    n_heads, nope, latent = ku.shape
    tree = q_ref.shape[0]
    per = q_ref.shape[1] // n_heads
    for copy in arriving:
        copy.wait()
    for h in range(n_heads):
        rows = pl.ds(h * tree, tree)
        q_nope = q_ref[:, h * per : h * per + nope]
        qs[rows, 0:latent] = dot(q_nope, ku[h]).astype(BF16)
        qs[rows, latent:] = q_ref[:, h * per + nope : (h + 1) * per]


def attend(fresh_ref, kt, vu, qs, ctx, heads, live, reach, arriving):
    n_heads, latent, value = vu.shape
    tree = fresh_ref.shape[0]
    scale = 1.0 / math.sqrt(value + qs.shape[1] - latent)
    for copy in arriving[:2]:
        copy.wait()
    block = 128
    pairs = kt.shape[0] // 2
    page = kt.shape[2]
    fresh = fresh_ref[...]
    allowed = jnp.concatenate([reach] * (block // tree), axis=0) > 0.5

    def body(i, carry):
        at = pl.multiple_of(i * block, block)
        q = qs[pl.ds(at, block), :]
        tree_score = jnp.where(allowed, dot(q, fresh, ((1,), (1,))) * scale, -1e30)
        scores = []
        for j in range(pairs):
            keys = jnp.concatenate([kt[2 * j], kt[2 * j + 1]], axis=1)
            mask = live[:, 2 * j * page : 2 * (j + 1) * page]
            scores.append(jnp.where(mask, dot(q, keys) * scale, -1e30))
        peak = jnp.max(tree_score, axis=1, keepdims=True)
        for s in scores:
            peak = jnp.maximum(peak, jnp.max(s, axis=1, keepdims=True))
        tree_score = jnp.exp(tree_score - peak)
        scores = [jnp.exp(s - peak) for s in scores]
        total = jnp.sum(tree_score, axis=1, keepdims=True)
        for s in scores:
            total = total + jnp.sum(s, axis=1, keepdims=True)
        inverse = 1.0 / total
        context = dot((tree_score * inverse).astype(BF16), fresh[:, 0:latent])
        for j in range(pairs):
            keys = jnp.concatenate([kt[2 * j, 0:latent], kt[2 * j + 1, 0:latent]], axis=1)
            context = context + dot((scores[j] * inverse).astype(BF16), keys, ((1,), (1,)))
        ctx[pl.ds(at, block), :] = context.astype(BF16)
        return carry

    lax.fori_loop(0, n_heads * tree // block, body, 0)
    arriving[2].wait()
    for h in range(n_heads):
        out = dot(ctx[pl.ds(h * tree, tree), :], vu[h])
        heads[0, :, h * vu.shape[2] : (h + 1) * vu.shape[2]] = out.astype(BF16)


def write_pages(kt, fresh_ref, path, offset, count):
    steps = fresh_ref.shape[0]
    step = lax.broadcasted_iota(jnp.int32, (steps, 1), 0)
    by_step = jnp.where(step == path, 1.0, 0.0).astype(BF16)
    page = kt.shape[2]
    for j in range(kt.shape[0]):
        here = offset[:, j * page : (j + 1) * page]
        at_step = jnp.where(step == here, 1.0, 0.0).astype(BF16)
        pick = dot(by_step, at_step).astype(BF16)
        rows = dot(fresh_ref[...], pick, ((0,), (0,))).astype(BF16)
        valid = jnp.where(jnp.logical_and(here >= 0, here < count), 1.0, 0.0)
        old = kt[j]
        kt[j] = jnp.where(jnp.broadcast_to(valid, old.shape) > 0.5, rows.astype(F32), old.astype(F32)).astype(BF16)


def layer_kernel(
    ptab_ref, clen_ref, count_ref,
    hid_hbm, q_hbm, fresh_hbm, parent_hbm, path_hbm, gain_hbm, ids_hbm, rw_hbm, const_hbm,
    pages_hbm, ku_hbm, vu_hbm, oproj_hbm, wg_hbm, wu_hbm, wd_hbm,
    out_ref, newp_hbm,
    hid_ref, q_ref, fresh_ref, parent_ref, path_ref, gain_ref, ids_ref, rw_ref, const_ref,
    kt, ku, vu, oproj, wg, wu, wd,
    qs, ctx, heads, po, co, mixed, routes, sel, wt, tok, ysend, x, accg, accu, act,
    p, a1, a3, bl, br, zz, v, zsend, zrecv,
    etok, eysend, ev, ezsend, ezrecv, exsend, exrecv,
    w_sem, h_s, h_r, o_s, o_r, tx_s, tx_r, t_s, t_r, fz_s, fz_r, fy_s, fy_r, fx_s, fx_r,
    gx_s, gx_r, gy_s, gy_r, gz_s, gz_r,
    efx_s, efx_r, efz_s, efz_r, efy_s, efy_r, egy_s, egy_r, egz_s, egz_r, egx_s, egx_r,
):
    rx = lax.axis_index("req")
    e = lax.axis_index("exp")
    ez = e // (2 * NY)
    ey = (e // 2) % NY
    ec = e % 2
    width = hid_ref.shape[1]
    cc = width // CHUNKS
    slots = ysend.shape[2]
    rows = x.shape[2]
    half = rows // 2
    tree = hid_ref.shape[0]

    def at_x(k):
        return ((rx + k) % NX, e)

    def at_z(k):
        return (rx, (((ez + k) % NZ) * NY + ey) * 2 + ec)

    def at_y(d):
        return (rx, (ez * NY + (ey + d // 2) % NY) * 2 + (ec + d % 2) % 2)

    def flip_y(d):
        return ((NY - d // 2) % NY) * 2 + d % 2

    in_copies = [
        pltpu.make_async_copy(src, dst, w_sem.at[n])
        for n, (src, dst) in enumerate(
            [
                (ids_hbm, ids_ref), (rw_hbm, rw_ref), (const_hbm, const_ref), (parent_hbm, parent_ref),
                (q_hbm, q_ref), (ku_hbm, ku), (pages_hbm, kt), (fresh_hbm, fresh_ref), (vu_hbm, vu),
                (oproj_hbm, oproj), (hid_hbm, hid_ref), (gain_hbm, gain_ref), (path_hbm, path_ref),
                (wg_hbm, wg), (wu_hbm, wu), (wd_hbm, wd),
            ]
        )
    ]
    for copy in in_copies:
        copy.start()
    hid_in, gain_in, path_in, wg_in, wu_in, wd_in = in_copies[10:]

    barrier = pltpu.get_barrier_semaphore()
    partners = (
        [at_x(k) for k in range(1, NX)]
        + [at_y(d) for d in range(1, 2 * NY)]
        + [at_z(k) for k in range(1, NZ)]
    )
    for partner in partners:
        pl.semaphore_signal(barrier, inc=1, device_id=partner, device_id_type=MESH)

    for copy in in_copies[:4]:
        copy.wait()
    routes[0, 0] = pack_routes(ids_ref, rw_ref, rx)
    page_len = kt.shape[2]
    n_pages = kt.shape[0]
    lane = lax.broadcasted_iota(jnp.int32, (1, page_len), 1)
    position = []
    for j in range(n_pages):
        logical = jnp.int32(0)
        for k in range(n_pages):
            logical = logical + jnp.where(ptab_ref[0, k] == j, k, 0)
        position.append(logical * page_len + lane)
    position = jnp.concatenate(position, axis=1)
    length = clen_ref[0]
    reach = ancestors(parent_ref[...], tree)

    started = []

    def send(src, dst, ss, rs, device):
        copy = pltpu.make_async_remote_copy(
            src_ref=src, dst_ref=dst, send_sem=ss, recv_sem=rs, device_id=device, device_id_type=MESH
        )
        copy.start()
        started.append(copy)
        return copy

    make_queries(q_ref, ku, qs, in_copies[4:6])
    attend(fresh_ref, kt, vu, qs, ctx, heads, position < length, reach, in_copies[6:9])
    pl.semaphore_wait(barrier, len(partners))

    route_copies = [
        send(routes.at[0, 0], routes.at[0, NX - k], tx_s.at[k], tx_r.at[NX - k], at_x(k)) for k in (1, 3, 2)
    ]
    head_copies = [
        send(heads.at[0], heads.at[NX - k], h_s.at[k], h_r.at[NX - k], at_x(k)) for k in (1, 3, 2)
    ]
    for copy in route_copies:
        copy.wait_recv()
    route_copies = [
        send(routes.at[0], routes.at[NZ - k], t_s.at[k], t_r.at[NZ - k], at_z(k)) for k in (1, 7, 2, 6, 3, 5, 4)
    ]
    for copy in in_copies[9:12]:
        copy.wait()
    for copy in head_copies:
        copy.wait_recv()
    proj = jnp.dot(heads[...].reshape(NX * tree, width), oproj[...], preferred_element_type=F32)
    po[...] = proj.astype(BF16).reshape(po.shape)
    back_copies = [send(po.at[k], co.at[rx], o_s.at[k], o_r.at[NX - k], at_x(k)) for k in (1, 3, 2)]
    co[rx] = po[0]
    for copy in route_copies:
        copy.wait_recv()

    def choose(g, carry):
        sel[g], wt[g] = selection(routes, g, ids_ref.shape[1], tree, const_ref, ez, ey, ec)
        return carry

    lax.fori_loop(0, NX, choose, 0)
    for copy in back_copies:
        copy.wait_recv()
    square = jnp.zeros((tree, 1), F32)
    for c in range(CHUNKS):
        per = width // NX
        at = c * cc % per
        column = co[c * cc // per, :, at : at + cc].astype(F32)
        m = (hid_ref[:, c * cc : (c + 1) * cc].astype(F32) + column).astype(BF16)
        mixed[c] = m
        mf = m.astype(F32)
        square = square + jnp.sum(mf * mf, axis=1, keepdims=True)
    factor = lax.rsqrt(square * (1.0 / width) + 1e-06)

    fz, fy, fx, fw = {}, {}, {}, {}
    efx, efz, efy = {}, {}, {}

    def normed(c):
        at = c * cc // 128
        gain = jnp.concatenate([gain_ref[n : n + 1, :] for n in range(at, at + cc // 128)], axis=1)
        return (mixed[c].astype(F32) * factor * gain.astype(F32)).astype(BF16)

    for b in range(EARLY):
        etok[b, 0, 0] = normed(LATE + b)
        efx[b] = [
            send(etok.at[b, 0, 0], etok.at[b, 0, NX - k], efx_s.at[b, k], efx_r.at[b, NX - k], at_x(k))
            for k in (1, 3, 2)
        ]

    near, far = (1, 7, 2, 6), (1, 7, 2, 6, 3, 5, 4)
    fr, efr = {}, {}

    def to_z(src, dst, ss, rs, steps):
        return [send(src, dst.at[NZ - k], ss.at[k], rs.at[NZ - k], at_z(k)) for k in steps]

    def relay(ref, ss, rs, copies):
        copies[2].wait_recv()
        copies[3].wait_recv()
        low, high = pl.ds(0, tree // 2), pl.ds(tree // 2, tree // 2)
        if len(ref.shape) == 3:
            parts = [ref.at[6, low], ref.at[4, low], ref.at[2, high], ref.at[4, high]]
        else:
            parts = [ref.at[6, :, low], ref.at[4, :, low], ref.at[2, :, high], ref.at[4, :, high]]
        return copies[:2] + [
            send(ref.at[6], ref.at[5], ss.at[3], rs.at[5], at_z(1)),
            send(ref.at[2], ref.at[3], ss.at[5], rs.at[3], at_z(7)),
            send(parts[0], parts[1], ss.at[4], rs.at[4], at_z(2)),
            send(parts[2], parts[3], ss.at[0], rs.at[0], at_z(6)),
        ]

    def spread_z(c):
        tok[c, 0] = normed(c)
        fz[c] = to_z(tok.at[c, 0], tok.at[c], fz_s.at[c], fz_r.at[c], near if c else far)

    def relay_z(c):
        fz[c] = relay(tok.at[c], fz_s.at[c], fz_r.at[c], fz[c])

    def early_z(b):
        for copy in efx[b]:
            copy.wait_recv()
        efz[b] = to_z(etok.at[b, 0], etok.at[b], efz_s.at[b], efz_r.at[b], near)

    def early_relay(b):
        efz[b] = relay(etok.at[b], efz_s.at[b], efz_r.at[b], efz[b])

    def early_select(b):
        for copy in efz[b]:
            copy.wait_recv()
        c = LATE + b

        def body(g, carry):
            block = dot(sel[g], etok[b, :, g].reshape(NZ * tree, cc)).astype(BF16)
            x[c, g, 0:slots] = block[0:slots]
            eysend[b, :, g] = block.reshape(2 * NY, slots, cc)
            return carry

        lax.fori_loop(0, NX, body, 0)
        efy[b] = [
            send(
                eysend.at[b, d],
                x.at[c, :, pl.ds(flip_y(d) * slots, slots)],
                efy_s.at[b, d],
                efy_r.at[b, flip_y(d)],
                at_y(d),
            )
            for d in (1, 2, 6, 3, 7, 4, 5)
        ]

    def select(c):
        for copy in fz[c]:
            copy.wait_recv()
        block = jnp.dot(sel[0], tok[c].reshape(NZ * tree, cc), preferred_element_type=F32)
        block = block.astype(BF16)
        x[c, 0, 0:slots] = block[0:slots]
        ysend[c] = block.reshape(2 * NY, slots, cc)
        fy[c] = [
            send(
                ysend.at[c, d],
                x.at[c, 0, pl.ds(flip_y(d) * slots, slots)],
                fy_s.at[c, d],
                fy_r.at[c, flip_y(d)],
                at_y(d),
            )
            for d in (1, 2, 6, 3, 7, 4, 5)
        ]

    def spread_x(c):
        for copy in fy[c]:
            copy.wait_recv()
        fx[c] = [
            send(x.at[c, 0], x.at[c, 3], fx_s.at[c, 0], fx_r.at[c, 0], at_x(1)),
            send(x.at[c, 0], x.at[c, 1], fx_s.at[c, 1], fx_r.at[c, 1], at_x(3)),
        ]

    def forward_x(c):
        top, bottom = pl.ds(0, half), pl.ds(half, half)
        fx[c][0].wait_recv()
        first = send(x.at[c, 3, top], x.at[c, 2, top], fx_s.at[c, 2], fx_r.at[c, 2], at_x(1))
        fx[c][1].wait_recv()
        second = send(x.at[c, 1, bottom], x.at[c, 2, bottom], fx_s.at[c, 3], fx_r.at[c, 3], at_x(3))
        fw[c] = [first, second]

    def expand(c, first, last):
        for copy in fw[c] if c < LATE else efy[c - LATE]:
            copy.wait_recv()
        if first:
            wg_in.wait()
            wu_in.wait()

        def body(g, carry):
            block = x[c, g]
            gv = dot(block, wg[:, c * cc : (c + 1) * cc], ((1,), (1,)))
            uv = dot(block, wu[:, c * cc : (c + 1) * cc], ((1,), (1,)))
            if not first:
                gv = gv + accg[g]
                uv = uv + accu[g]
            if last:
                act[g] = (gv * jax.nn.sigmoid(gv) * uv).astype(BF16)
            else:
                accg[g] = gv
                accu[g] = uv
            return carry

        lax.fori_loop(0, NX, body, 0)

    for c in range(LATE):
        spread_z(c)
    for i in range(LATE + 3):
        if i < LATE:
            select(i)
        for c in (2 * i + 1, 2 * i + 2):
            if c < LATE:
                relay_z(c)
        for b in range(EARLY):
            if i == EARLY_Z_AT[b]:
                early_z(b)
            if i == EARLY_RELAY_AT[b]:
                early_relay(b)
        if 0 <= i - 1 < LATE:
            spread_x(i - 1)
        if 0 <= i - 2 < LATE:
            forward_x(i - 2)
        for b in range(EARLY):
            if i == SELECT_AT[b]:
                early_select(b)
        if 0 <= i - 3 < LATE:
            expand(i - 3, i == 3, i == LATE + 2 and EXPAND_AT[-1] != i)
        for b in range(EARLY):
            if i == EXPAND_AT[b]:
                expand(LATE + b, False, i == LATE + 2 and b == EARLY - 1)
        if i == 2:
            path_in.wait()
            write_pages(kt, fresh_ref, path_ref[...], position - length, count_ref[0])
            page_out = pltpu.make_async_copy(kt, newp_hbm, w_sem.at[16])
            page_out.start()

    wd_in.wait()
    gx, gw, gy, gz = {}, {}, {}, {}
    egy, egz, egx = {}, {}, {}

    def contract(c):
        top, bottom = pl.ds(0, half), pl.ds(half, half)

        def body(j, carry):
            g = (3 + j) % NX
            p[c, g] = dot(act[g], wd[:, c * cc : (c + 1) * cc]).astype(BF16)
            return carry

        if c < LATE:
            body(3, 0)
            gx[c] = [
                send(p.at[c, 2, top], a1.at[c], gx_s.at[c, 0], gx_r.at[c, 0], at_x(1)),
                send(p.at[c, 2, bottom], a3.at[c], gx_s.at[c, 1], gx_r.at[c, 1], at_x(3)),
            ]
            lax.fori_loop(0, 3, body, 0)
        else:
            b = c - LATE
            lax.fori_loop(0, 4, body, 0)
            egy[b] = [
                send(
                    p.at[c, :, pl.ds(d * slots, slots)], ev.at[b, flip_y(d)],
                    egy_s.at[b, d], egy_r.at[b, flip_y(d)], at_y(d),
                )
                for d in (1, 2, 6, 3, 7, 4, 5)
            ]
            ev[b, 0] = p[c, :, 0:slots]

    def back_start(src, dst, ss, rs):
        low, high = pl.ds(0, tree // 2), pl.ds(tree // 2, tree // 2)
        if len(src.shape) == 3:
            parts = [src.at[4, low], dst.at[4, low], src.at[4, high], dst.at[4, high]]
        else:
            parts = [src.at[4, :, low], dst.at[4, :, low], src.at[4, :, high], dst.at[4, :, high]]
        return [
            send(src.at[3], dst.at[3], ss.at[3], rs.at[3], at_z(1)),
            send(src.at[5], dst.at[5], ss.at[5], rs.at[5], at_z(7)),
            send(parts[0], parts[1], ss.at[4], rs.at[4], at_z(2)),
            send(parts[2], parts[3], ss.at[0], rs.at[0], at_z(6)),
            send(src.at[1], dst.at[7], ss.at[1], rs.at[7], at_z(1)),
            send(src.at[7], dst.at[1], ss.at[7], rs.at[1], at_z(7)),
        ]

    def back_relay(src, dst, ss, rs, copies):
        for copy in copies[:4]:
            copy.wait_recv()
        cut = tree // 2
        src[2] = (src[2].astype(F32) + dst[3].astype(F32)).astype(BF16)
        src[6] = (src[6].astype(F32) + dst[5].astype(F32)).astype(BF16)
        if len(src.shape) == 3:
            src[2, 0:cut] = (src[2, 0:cut].astype(F32) + dst[4, 0:cut].astype(F32)).astype(BF16)
            src[6, cut:] = (src[6, cut:].astype(F32) + dst[4, cut:].astype(F32)).astype(BF16)
        else:
            src[2, :, 0:cut] = (src[2, :, 0:cut].astype(F32) + dst[4, :, 0:cut].astype(F32)).astype(BF16)
            src[6, :, cut:] = (src[6, :, cut:].astype(F32) + dst[4, :, cut:].astype(F32)).astype(BF16)
        return copies[4:] + [
            send(src.at[2], dst.at[6], ss.at[2], rs.at[6], at_z(2)),
            send(src.at[6], dst.at[2], ss.at[6], rs.at[2], at_z(6)),
        ]

    def early_back_z(b):
        for copy in egy[b]:
            copy.wait_recv()

        def body(g, carry):
            part = dot(wt[g], ev[b, :, g].reshape(rows, cc))
            ezsend[b, :, g] = part.astype(BF16).reshape(NZ, tree, cc)
            return carry

        lax.fori_loop(0, NX, body, 0)
        egz[b] = back_start(ezsend.at[b], ezrecv.at[b], egz_s.at[b], egz_r.at[b])

    def early_back_relay(b):
        egz[b] = back_relay(ezsend.at[b], ezrecv.at[b], egz_s.at[b], egz_r.at[b], egz[b])

    def early_back_x(b):
        for copy in egz[b]:
            copy.wait_recv()
        total = ezsend[b, 0].astype(F32)
        for k in near:
            total = total + ezrecv[b, k].astype(F32)
        exsend[b] = total.astype(BF16)
        egx[b] = [
            send(exsend.at[b, k], exrecv.at[b, NX - k], egx_s.at[b, k], egx_r.at[b, NX - k], at_x(k))
            for k in (1, 3, 2)
        ]

    def early_finish(b):
        for copy in egx[b]:
            copy.wait_recv()
        c = LATE + b
        total = mixed[c].astype(F32) + exsend[b, 0].astype(F32)
        for k in range(1, NX):
            total = total + exrecv[b, k].astype(F32)
        out_ref[:, c * cc : (c + 1) * cc] = total.astype(BF16)

    def gather_x(c):
        gx[c][0].wait_recv()
        p[c, 1, 0:half] = (p[c, 1, 0:half].astype(F32) + a1[c].astype(F32)).astype(BF16)
        first = send(p.at[c, 1], bl.at[c], gx_s.at[c, 2], gx_r.at[c, 2], at_x(1))
        gx[c][1].wait_recv()
        p[c, 3, half:rows] = (p[c, 3, half:rows].astype(F32) + a3[c].astype(F32)).astype(BF16)
        second = send(p.at[c, 3], br.at[c], gx_s.at[c, 3], gx_r.at[c, 3], at_x(3))
        gw[c] = [first, second]

    def back_y(c):
        for copy in gw[c]:
            copy.wait_recv()
        total = p[c, 0].astype(F32) + bl[c].astype(F32) + br[c].astype(F32)
        total = total.astype(BF16).reshape(2 * NY, slots, cc)
        v[c, 0] = total[0]
        zz[c] = total
        gy[c] = [
            send(zz.at[c, d], v.at[c, flip_y(d)], gy_s.at[c, d], gy_r.at[c, flip_y(d)], at_y(d))
            for d in (1, 2, 6, 3, 7, 4, 5)
        ]

    def back_z(c):
        for copy in gy[c]:
            copy.wait_recv()
        part = dot(wt[0], v[c].reshape(rows, cc))
        zsend[c] = part.astype(BF16).reshape(NZ, tree, cc)
        if c < LATE - 1:
            gz[c] = back_start(zsend.at[c], zrecv.at[c], gz_s.at[c], gz_r.at[c])
        else:
            gz[c] = [
                send(zsend.at[c, k], zrecv.at[c, NZ - k], gz_s.at[c, k], gz_r.at[c, NZ - k], at_z(k)) for k in far
            ]

    def relay_back(c):
        if c < LATE - 1:
            gz[c] = back_relay(zsend.at[c], zrecv.at[c], gz_s.at[c], gz_r.at[c], gz[c])

    def finish(c):
        for copy in gz[c]:
            copy.wait_recv()
        total = mixed[c].astype(F32) + zsend[c, 0].astype(F32)
        for k in near if c < LATE - 1 else far:
            total = total + zrecv[c, k].astype(F32)
        out_ref[:, c * cc : (c + 1) * cc] = total.astype(BF16)

    for i in range(LATE + 4):
        if i < LATE:
            contract(i)
        if 0 <= i - 1 < LATE:
            gather_x(i - 1)
        for b in range(EARLY):
            if i == CONTRACT_AT[b]:
                contract(LATE + b)
        if 0 <= i - 2 < LATE:
            back_y(i - 2)
        if 0 <= i - 3 < LATE:
            back_z(i - 3)
        if 0 <= i - 4 < LATE:
            relay_back(i - 4)
        for b in range(EARLY):
            if i == BACK_Z_AT[b]:
                early_back_z(b)
            if i == BACK_RELAY_AT[b]:
                early_back_relay(b)
            if i == BACK_X_AT[b]:
                early_back_x(b)
        if 0 <= i - 5 < LATE:
            finish(i - 5)
    finish(LATE - 1)
    for b in range(EARLY):
        early_finish(b)

    for copy in started:
        copy.wait_send()
    page_out.wait()


def constants(cap):
    slots = 2 * NY * cap
    i = np.arange(NZ * slots)
    table = np.zeros((NZ * slots, 128), np.int32)
    for n, column in enumerate((i // slots, (i % slots) // cap, i % cap)):
        table[:, n] = column
    return table


def run_layer(
    hidden, queries, fresh, pages_t, page_table, cache_len, parents, accept_path, accept_count,
    key_up, value_up, out_proj, gain, ids, weights, wg_t, wu_t, w_down,
):
    tree, width = hidden.shape
    cc = width // CHUNKS
    hid = w_down.shape[0]
    n_heads = key_up.shape[0]
    cap = max(2, min(tree, 2 * tree * ids.shape[1] // (NZ * NY * 2)))
    slots = 2 * NY * cap
    rows = NZ * slots
    cols = NZ * tree
    smem = pl.BlockSpec(memory_space=pltpu.SMEM)
    vmem = pl.BlockSpec(memory_space=pltpu.VMEM)
    hbm = pl.BlockSpec(memory_space=pl.ANY)
    dma = pltpu.SemaphoreType.DMA
    c = CHUNKS
    staged = [
        hidden, queries, fresh, parents, accept_path, gain, ids, weights, jnp.asarray(constants(cap)),
        pages_t, key_up, value_up, out_proj, wg_t, wu_t, w_down,
    ]
    return pl.pallas_call(
        layer_kernel,
        out_shape=(jax.ShapeDtypeStruct((tree, width), BF16), jax.ShapeDtypeStruct(pages_t.shape, BF16)),
        in_specs=[smem] * 3 + [hbm] * 16,
        out_specs=(vmem, hbm),
        scratch_shapes=[pltpu.VMEM(value.shape, value.dtype) for value in staged]
        + [
            pltpu.VMEM(shape, dtype)
            for shape, dtype in (
                ((n_heads * tree, fresh.shape[1]), BF16),
                ((n_heads * tree, key_up.shape[2]), BF16),
                ((NX, tree, width), BF16),
                ((NX, tree, width // NX), BF16),
                ((NX, tree, width // NX), BF16),
                ((c, tree, cc), BF16),
                ((NZ, NX, 16, 128), BF16),
                ((NX, rows, cols), BF16),
                ((NX, cols, rows), BF16),
                ((LATE, NZ, tree, cc), BF16),
                ((LATE, 2 * NY, slots, cc), BF16),
                ((c, NX, rows, cc), BF16),
                ((NX, rows, hid), F32),
                ((NX, rows, hid), F32),
                ((NX, rows, hid), BF16),
                ((c, NX, rows, cc), BF16),
                ((LATE, rows // 2, cc), BF16),
                ((LATE, rows // 2, cc), BF16),
                ((LATE, rows, cc), BF16),
                ((LATE, rows, cc), BF16),
                ((LATE, 2 * NY, slots, cc), BF16),
                ((LATE, 2 * NY, slots, cc), BF16),
                ((LATE, NZ, tree, cc), BF16),
                ((LATE, NZ, tree, cc), BF16),
                ((EARLY, NZ, NX, tree, cc), BF16),
                ((EARLY, 2 * NY, NX, slots, cc), BF16),
                ((EARLY, 2 * NY, NX, slots, cc), BF16),
                ((EARLY, NZ, NX, tree, cc), BF16),
                ((EARLY, NZ, NX, tree, cc), BF16),
                ((EARLY, NX, tree, cc), BF16),
                ((EARLY, NX, tree, cc), BF16),
            )
        ]
        + [
            dma(shape)
            for shape in [(17,)]
            + [(NX,)] * 6
            + [(NZ,)] * 2
            + [(LATE, NZ)] * 2
            + [(LATE, 2 * NY)] * 2
            + [(LATE, 4)] * 4
            + [(LATE, 2 * NY)] * 2
            + [(LATE, NZ)] * 2
            + [(EARLY, NX)] * 2
            + [(EARLY, NZ)] * 2
            + [(EARLY, 2 * NY)] * 4
            + [(EARLY, NZ)] * 2
            + [(EARLY, NX)] * 2
        ],
        compiler_params=pltpu.CompilerParams(
            collective_id=0, has_side_effects=True, vmem_limit_bytes=60 * 1024 * 1024
        ),
        name="layer",
    )(page_table, cache_len, accept_count, *staged)


def local(
    hidden, queries, new_latent, pages, page_table, cache_len, parents, accept_path, accept_count,
    key_up, value_up, out_proj, norm_gain, route_ids, route_weights, w_gate, w_up, w_down,
):
    layer_out, pages_out = run_layer(
        hidden[0], queries[0], new_latent[0], jnp.swapaxes(pages, 1, 2), page_table, cache_len, parents,
        accept_path, accept_count, key_up, value_up, out_proj, norm_gain.reshape(-1, 128),
        jnp.transpose(route_ids, (0, 3, 1, 2)), jnp.transpose(route_weights, (0, 3, 1, 2)),
        jnp.swapaxes(w_gate[0], 0, 1), jnp.swapaxes(w_up[0], 0, 1), w_down[0],
    )
    return (layer_out[None], jnp.swapaxes(pages_out, 1, 2))


def solution(mesh):
    in_specs = (
        P(("req", "exp"), None, None),
        P(("req", "exp"), None, None),
        P(("req", "exp"), None, None),
        P(("req", "exp"), None, None),
        P(("req", "exp"), None),
        P(("req", "exp")),
        P(("req", "exp"), None),
        P(("req", "exp"), None),
        P(("req", "exp")),
        P(),
        P(),
        P(None, "req"),
        P(),
        P(None, "exp", None, None),
        P(None, "exp", None, None),
        P("exp", None, "req"),
        P("exp", None, "req"),
        P("exp", "req", None),
    )
    out_specs = (P(("req", "exp"), None, None), P(("req", "exp"), None, None))
    return jax.shard_map(local, mesh=mesh, in_specs=in_specs, out_specs=out_specs, check_vma=False)
```

time: 177 us -> 158 us (0.89)
  Pallas kernels: 167 us -> 152 us
  local copies, waits for them, and re-layouts: 7.86 us -> 3.94 us
    pallas_call x1, Pallas kernels: 167 us -> 152 us  [run_layer(): pl.pallas_call(layer_kernel, out_shape=(jax.ShapeDtypeStruct((tree, width...]
    unnamed x4 -> x2, local copies, waits for them, and re-layouts: 5.36 us -> 3.94 us
where the time goes in v3:
time: 158 us
  Pallas kernels  152 us (96%)
  local copies, waits for them, and re-layouts  3.94 us (2%)
  between operations  1.94 us (1%)
    pallas_call x1, Pallas kernels, run_layer(): pl.pallas_call(layer_kernel, out_shape=(jax.ShapeDtypeStruct((tree, width...  152 us
    unnamed x2, local copies, waits for them, and re-layouts  3.94 us

profile of v3, /device:TPU:1, one launch (start us, length us, event | category | flops | bytes accessed | tf_op | source)
XLA Modules:
  0.0 158.0 jit_solution(14943239836111321578)
XLA Ops:
  1.9 152.1 %layer.1 = (bf16[32,2048]{1,0:T(8,128)(2,1)}, bf16[8,576,128]{2,1,0:T(8,128)(2,1)}) custom-call(s32[1,8]{1,0:T(1,128)} %ptab_ref.1, s32[1]{0:T(128)S(6)} %copy.23.clen_ref, s32[1]{0:T(128)S(6)} %copy.24.count_ref, bf16[32,2048]{1,0:T(8,128)(2,1)} %bitcast.22, bf16[32,3072]{1,0:T(8,128)(2,1)} %bitcast.21, bf16[32,576]{1,0:T(8,128)(2,1)} %bitcast.24, ...), custom_call_target="tpu_custom_call" | custom-call | tf_op jit(solution)/shard_map/layer/pallas_call | solution.py:653
  154.0 1.6 copy.25
  155.6 2.4 %copy.26 = bf16[8,128,576]{1,2,0:T(8,128)(2,1)} copy(bf16[8,128,576]{1,2,0:T(8,128)(2,1)} %bitcast.20) | data formatting | bytes 2359296
